TPU v7x, 256 devices: a whole 4x4x8 slice. The times are simulated.
256 devices in a mesh: dp: 8 (over x, core), expert: 32 (over z, y).
Axes of the slice: x: 4, y: 4, z: 8, core: 2. Of those that a mesh axis runs over, the one named last changes fastest.
Arguments:
- tokens: bfloat16 [8192, 7168], P('expert', 'dp'), may hold values from -6 to 6
- grad_out: bfloat16 [8192, 7168], P('expert', 'dp'), may hold values from -6 to 6
- route_ids: int32 [8192, 8], P('expert'), may hold values from 0 to 255, all different within a row; in each aligned block of 256 rows (0 to 255, 256 to 511, ...) at most 12 rows name the same one
- route_gates: float32 [8192, 8], P('expert'), may hold values from 0.1 to 1
- w_gate: bfloat16 [32, 7168, 1024], P('expert', 'dp'), may hold values from -0.0625 to 0.0625
- w_up: bfloat16 [32, 7168, 1024], P('expert', 'dp'), may hold values from -0.0625 to 0.0625
- w_down: bfloat16 [32, 1024, 7168], P('expert', None, 'dp'), may hold values from -0.1875 to 0.1875
- shared_gate: bfloat16 [7168, 1024], P('dp', 'expert'), may hold values from -0.0625 to 0.0625
- shared_up: bfloat16 [7168, 1024], P('dp', 'expert'), may hold values from -0.0625 to 0.0625
- shared_down: bfloat16 [1024, 7168], P('expert', 'dp'), may hold values from -0.1875 to 0.1875
Outputs:
- grad_tokens: bfloat16 [8192, 7168], P('expert', 'dp')
- grad_gate: bfloat16 [32, 7168, 1024], P('expert', 'dp')
- grad_up: bfloat16 [32, 7168, 1024], P('expert', 'dp')
- grad_down: bfloat16 [32, 1024, 7168], P('expert', None, 'dp')
- grad_shared_gate: float32 [7168, 1024], P('dp', 'expert')
- grad_shared_up: float32 [7168, 1024], P('dp', 'expert')
- grad_shared_down: float32 [1024, 7168], P('expert', 'dp')
Inputs may be any that keep to these rules, and one draw needn't show every extreme that they name: `route_ids`: each row names 8 different experts; in each aligned block of 256 rows no expert is named by more than 12 rows, a bound that some block reaches.
All inputs are finite; a program needn't handle non-finite values.
Results may differ from a plain program's by a relative error of at most 0.018.
Values may be sent and summed in bfloat16 or wider, within the bound.
No kernel may reach another device: no remote copies, remote signals or barrier semaphores. Data moves between devices by JAX's collectives and lax.ppermute only.
A program may use at most 128 MiB of HBM per device.

v0:
```python
import jax
import jax.numpy as jnp
from jax import lax
from jax.experimental import pallas as pl
from jax.experimental.pallas import tpu as pltpu
from jax.sharding import Mesh
from jax.sharding import PartitionSpec as P

CAP = 12
NY = 4
BF16 = jnp.bfloat16
F32 = jnp.float32


def silu_parts(pre):
    sigmoid_val = jax.nn.sigmoid(pre)
    return (pre * sigmoid_val, sigmoid_val * (1.0 + pre * (1.0 - sigmoid_val)))


def dot_rows(left, right):
    return lax.dot_general(left, right, (((0,), (0,)), ((), ())), preferred_element_type=F32)


def dot_cols(left, right):
    return lax.dot_general(left, right, (((1,), (1,)), ((), ())), preferred_element_type=F32)


def dot(left, right):
    return jnp.dot(left, right, preferred_element_type=F32)


def hidden_products(part_gate, part_up, part_act):
    silu_val, silu_slope = silu_parts(part_gate)
    activated = (silu_val * part_up).astype(BF16)
    grad_gate_pre = (part_act * part_up * silu_slope).astype(BF16)
    grad_up_pre = (part_act * silu_val).astype(BF16)
    return (activated, grad_gate_pre, grad_up_pre)


def shift(value, axis, by):
    size = lax.axis_size(axis)
    return lax.ppermute(value, axis, [(i, (i + by) % size) for i in range(size)])


def pick(value, index, axis):
    return lax.dynamic_index_in_dim(value, index, axis, keepdims=False)


def x_pieces(kept, got):
    n_x, x = lax.axis_size("x"), lax.axis_index("x")
    summed = (kept + got.astype(F32)).reshape(n_x, kept.shape[0] // n_x, kept.shape[1])
    return pick(summed, x, 0), [pick(summed, (x + j) & (n_x - 1), 0).astype(BF16) for j in range(1, n_x)]


def x_sum(own, pieces):
    for j, piece in enumerate(pieces):
        own = own + shift(piece, "x", j + 1).astype(F32)
    return own


def gather_blocks(value, along=()):
    n_x = lax.axis_size("x")
    mine = [value] + [shift(value, "x", -j) for j in range(1, n_x)]
    mine[2], along = lax.optimization_barrier((mine[2], along))
    return mine + [shift(block, "core", 1) for block in mine], along


def place_kernel(where, *refs):
    *blocks, out = refs
    n_core, n_x = out.shape[:2]
    for i, block in enumerate(blocks):
        out[(where[1] + i // n_x) & (n_core - 1), (where[0] + i % n_x) & (n_x - 1)] = block[...]


def place_blocks(blocks, where):
    n_x = lax.axis_size("x")
    rows, cols = blocks[0].shape
    out = pl.pallas_call(
        place_kernel,
        out_shape=jax.ShapeDtypeStruct((2, n_x, rows, cols), blocks[0].dtype),
        in_specs=[pl.BlockSpec(memory_space=pltpu.SMEM)] + [pl.BlockSpec(memory_space=pltpu.VMEM)] * len(blocks),
        out_specs=pl.BlockSpec(memory_space=pltpu.VMEM),
        compiler_params=pltpu.CompilerParams(vmem_limit_bytes=2 << 20),
        cost_estimate=pl.CostEstimate(flops=0, bytes_accessed=8 * n_x * rows * cols, transcendentals=0),
        name="place_blocks",
    )(where, *blocks)
    return out.reshape(2 * n_x * rows, cols)


def part_kernel(where, tok, grd, weights, send, kept):
    step = pl.program_id(0)
    units = weights.shape[1] // 3
    width = weights.shape[2]
    sh = weights.shape[0] * units
    gate, up, down = (weights[:, k * units : (k + 1) * units].reshape(sh, width) for k in range(3))
    part = [dot_cols(tok[0, 0], gate), dot_cols(tok[0, 0], up), dot_cols(grd[0, 0], down)]

    @pl.when(step < 2)
    def _():
        for k in range(3):
            send[:, k * sh : (k + 1) * sh] = part[k].astype(BF16)

    @pl.when(step >= 2)
    def _():
        for k in range(3):
            kept[:, k * sh : (k + 1) * sh] = part[k]


def shared_partials(where, group, weights):
    n_y, _, n_tok, width = group.shape
    cols = weights.shape[0] * weights.shape[1]
    rows = [
        pl.BlockSpec((1, 1, n_tok, width), lambda i, where, k=k: ((i + 2 * (1 - where[1])) & 3, k, 0, 0)) for k in (0, 1)
    ]
    return pl.pallas_call(
        part_kernel,
        out_shape=(
            jax.ShapeDtypeStruct((2 * n_tok, cols), BF16),
            jax.ShapeDtypeStruct((2 * n_tok, cols), F32),
        ),
        grid_spec=pltpu.PrefetchScalarGridSpec(
            num_scalar_prefetch=1,
            grid=(n_y,),
            in_specs=[*rows, pl.BlockSpec(weights.shape, lambda i, where: (0, 0, 0), pipeline_mode=pl.Buffered(1))],
            out_specs=[
                pl.BlockSpec((n_tok, cols), lambda i, where: (jnp.minimum(i, 1), 0)),
                pl.BlockSpec((n_tok, cols), lambda i, where: (jnp.maximum(i - 2, 0), 0)),
            ],
        ),
        compiler_params=pltpu.CompilerParams(vmem_limit_bytes=11 << 20),
        cost_estimate=pl.CostEstimate(
            flops=2 * n_y * n_tok * width * cols, bytes_accessed=4 * n_y * n_tok * width, transcendentals=0
        ),
        name="shared_partials",
    )(where, group, group, weights)


def back_kernel(scale, products, tok, grd, weights, mine, back, own):
    step = pl.program_id(0)
    nz, units, width = weights.shape[0], weights.shape[1] // 3, weights.shape[2]
    sh = nz * units
    gate, up = (weights[:, k * units : (k + 1) * units].reshape(sh, width) for k in range(2))
    act, d_gate, d_up = (products[:, k * sh : (k + 1) * sh] for k in range(3))
    total = dot(d_gate, gate) + dot(d_up, up)
    back[0] = total.astype(BF16)

    @pl.when(step == 0)
    def _():
        mine[...] = total

    grads = [dot_rows(d_gate, tok[0, 0]), dot_rows(d_up, tok[0, 0]), dot_rows(act, grd[0, 0])]

    @pl.when(step == 0)
    def _():
        for k in range(3):
            own[:, k * units : (k + 1) * units] = (grads[k] * scale).reshape(nz, units, width)

    @pl.when(step > 0)
    def _():
        for k in range(3):
            own[:, k * units : (k + 1) * units] += (grads[k] * scale).reshape(nz, units, width)


def shared_back(products, group, weights, scale):
    n_y, _, n_tok, width = group.shape
    rows = [pl.BlockSpec((1, 1, n_tok, width), lambda i, k=k: (i, k, 0, 0)) for k in (0, 1)]
    whole = pl.BlockSpec(weights.shape, lambda i: (0, 0, 0), pipeline_mode=pl.Buffered(1))
    cols = products.shape[1]
    return pl.pallas_call(
        lambda *refs: back_kernel(scale, *refs),
        out_shape=(
            jax.ShapeDtypeStruct((n_tok, width), F32),
            jax.ShapeDtypeStruct((n_y, n_tok, width), BF16),
            jax.ShapeDtypeStruct(weights.shape, F32),
        ),
        grid=(n_y,),
        in_specs=[pl.BlockSpec((n_tok, cols), lambda i: (i, 0)), *rows, whole],
        out_specs=[pl.BlockSpec((n_tok, width), lambda i: (0, 0), pipeline_mode=pl.Buffered(1)), pl.BlockSpec((1, n_tok, width), lambda i: (i, 0, 0)), whole],
        compiler_params=pltpu.CompilerParams(vmem_limit_bytes=16 << 20),
        cost_estimate=pl.CostEstimate(
            flops=10 * n_y * n_tok * width * cols // 3, bytes_accessed=8 * n_y * n_tok * width, transcendentals=0
        ),
        name="shared_back",
    )(products, group, group, weights)


def routed_kernel(where, compact, recv, w_gate, w_up, w_down, rows, send, kept):
    step = pl.program_id(0)
    n_rows, tile = rows.shape[0] // 2, w_gate.shape[2]
    half = n_rows // 2
    hid = send.shape[1] // 3

    @pl.when(step == 0)
    def _():
        rows[...] = dot(compact[...], recv[...]).astype(BF16)

    def ordered(base):
        return jnp.concatenate(
            [
                rows[pl.ds(pl.multiple_of(base + (1 - where[1]) * half, half), half)],
                rows[pl.ds(pl.multiple_of(base + where[1] * half, half), half)],
            ],
            axis=0,
        )

    rows_in, rows_grad = ordered(0), ordered(n_rows)
    part = [dot(rows_in, w_gate[0]), dot(rows_in, w_up[0]), dot_cols(rows_grad, w_down[0])]
    for k in range(3):
        spot = pl.ds(pl.multiple_of(k * hid + step * tile, tile), tile)
        send[:, spot] = part[k][:half].astype(BF16)
        kept[:, spot] = part[k][half:]


def routed_partials(where, compact, recv, w_gate, w_up, w_down):
    n_rows = recv.shape[0] // 2
    width, hid = w_gate.shape[1:]
    tile = min(256, hid)
    whole = lambda shape: pl.BlockSpec(shape, lambda i, where: (0,) * len(shape), pipeline_mode=pl.Buffered(1))
    out = [
        jax.ShapeDtypeStruct((2 * n_rows, width), BF16),
        jax.ShapeDtypeStruct((n_rows // 2, 3 * hid), BF16),
        jax.ShapeDtypeStruct((n_rows // 2, 3 * hid), F32),
    ]
    return pl.pallas_call(
        routed_kernel,
        out_shape=out,
        grid_spec=pltpu.PrefetchScalarGridSpec(
            num_scalar_prefetch=1,
            grid=(hid // tile,),
            in_specs=[
                whole(compact.shape),
                whole(recv.shape),
                pl.BlockSpec((1, width, tile), lambda i, where: (0, 0, i)),
                pl.BlockSpec((1, width, tile), lambda i, where: (0, 0, i)),
                pl.BlockSpec((1, tile, width), lambda i, where: (0, i, 0)),
            ],
            out_specs=[whole(o.shape) for o in out],
        ),
        compiler_params=pltpu.CompilerParams(vmem_limit_bytes=14 << 20),
        cost_estimate=pl.CostEstimate(
            flops=6 * n_rows * width * hid, bytes_accessed=6 * width * hid, transcendentals=0
        ),
        name="routed_partials",
    )(where, compact, recv, w_gate, w_up, w_down)


def shards(tokens, grad_out, route_ids, route_gates, w_gate, w_up, w_down, shared_gate, shared_up, shared_down):
    n_z, n_y, n_x = lax.axis_size("z"), lax.axis_size("y"), lax.axis_size("x")
    n_exp = n_z * n_y
    scale = 1.0 / n_exp
    n_tok, width = tokens.shape
    hid = w_gate.shape[2]
    units = shared_down.shape[0]
    sh = n_z * units
    n_rows = n_exp * CAP

    own_w = jnp.concatenate([shared_gate.T, shared_up.T, shared_down], axis=0)
    all_w = lax.all_gather(own_w, "z", axis=0, tiled=True)

    both = jnp.stack([tokens, grad_out])
    up, down = shift(both, "y", 1), shift(both, "y", -1)

    experts = jnp.arange(n_exp, dtype=jnp.int32)[:, None]
    ids, gates = route_ids.T, route_gates.T
    chosen = jnp.zeros((n_exp, n_tok), jnp.bool_)
    gate_total = jnp.zeros((n_exp, n_tok), F32)
    for k in range(ids.shape[0]):
        match = ids[k : k + 1] == experts
        chosen = chosen | match
        gate_total = gate_total + jnp.where(match, gates[k : k + 1], 0.0)
    spots = jnp.arange(n_tok, dtype=jnp.int32)
    earlier = (spots[:, None] < spots[None, :]).astype(BF16)
    rank = dot(chosen.astype(BF16), earlier)
    rank = jnp.where(chosen, rank, -1.0)
    slots = jnp.arange(2 * CAP, dtype=jnp.int32)[None, :, None]
    rank_in = jnp.where(slots < CAP, rank.astype(jnp.int32)[:, None, :], -1) == slots
    rank_grad = jnp.where(slots >= CAP, rank.astype(jnp.int32)[:, None, :] + CAP, -1) == slots
    rank_grad = rank_grad & chosen[:, None, :]
    slot_gate = jnp.sum(jnp.where(rank_grad, gate_total[:, None, :], 0.0), axis=2)
    slot_gate = jnp.where(slots[0, :, 0][None, :] < CAP, 1.0, slot_gate)
    picked = dot(rank_in.astype(BF16).reshape(2 * n_rows, n_tok), tokens)
    picked = picked + dot(rank_grad.astype(BF16).reshape(2 * n_rows, n_tok), grad_out)
    send = (picked.reshape(n_exp, 2 * CAP, width) * slot_gate[:, :, None]).astype(BF16)
    send, up, down, _ = lax.optimization_barrier((send, up, down, own_w))
    recv = lax.all_to_all(send, ("z", "y"), split_axis=0, concat_axis=0, tiled=True)

    where = jnp.stack([lax.axis_index("x"), lax.axis_index("core")]).astype(jnp.int32)
    spot = jnp.arange(2 * n_rows, dtype=jnp.int32)
    spot = (spot % n_rows) // CAP * (2 * CAP) + spot % CAP + spot // n_rows * CAP
    compact = (spot[:, None] == jnp.arange(2 * n_rows, dtype=jnp.int32)[None, :]).astype(BF16)
    compact = lax.optimization_barrier(compact)

    all_w = all_w.reshape(n_z, 3 * units, width)
    far = n_tok // 2
    group = jnp.zeros((n_y,) + both.shape, BF16)
    for i, part in ((0, both), (1, up), (n_y - 1, down)):
        group = lax.dynamic_update_slice(group, part[None], (i, 0, 0, 0))
    group = lax.dynamic_update_slice(group, shift(up[:, :far], "y", 1)[None], (2, 0, 0, 0))
    group = lax.dynamic_update_slice(group, shift(down[:, far:], "y", -1)[None], (2, 0, far, 0))
    s_send, s_kept = shared_partials(where, group, all_w)
    s_own, s_pieces = x_pieces(s_kept, shift(s_send, "core", 1))
    rows_all, r_send, r_kept = routed_partials(
        where, compact, recv.reshape(2 * n_rows, width), w_gate, w_up, w_down
    )
    rows_in, rows_grad = rows_all[:n_rows], rows_all[n_rows:]
    r_own, r_pieces = x_pieces(r_kept, shift(r_send, "core", 1))
    s_total = x_sum(s_own, s_pieces)
    s_total, *r_pieces = lax.optimization_barrier((s_total, *r_pieces))
    s_blocks, _ = gather_blocks(
        jnp.concatenate(hidden_products(s_total[:, :sh], s_total[:, sh : 2 * sh], s_total[:, 2 * sh :]), axis=1)
    )
    r_total = x_sum(r_own, r_pieces)
    r_products = jnp.concatenate(
        hidden_products(r_total[:, :hid], r_total[:, hid : 2 * hid], r_total[:, 2 * hid :]), axis=1
    )

    s_products, r_products = lax.optimization_barrier((place_blocks(s_blocks, where), r_products))
    mine, s_back, own = shared_back(s_products, group, all_w, scale)
    y_got = [shift(s_back[j], "y", -j) for j in range(1, n_y)]
    r_blocks, y_got = gather_blocks(r_products, y_got)
    for got in y_got:
        mine = mine + got.astype(F32)
    own = lax.psum_scatter(own.reshape(n_z * 3 * units, width), "z", scatter_dimension=0, tiled=True)
    own = own.reshape(3, units, width)

    products = place_blocks(r_blocks, where)
    r_act, r_gate, r_up = (products[:, k * hid : (k + 1) * hid] for k in range(3))
    back = (dot_cols(r_gate, w_gate[0]) + dot_cols(r_up, w_up[0])).astype(BF16)
    back_rows = lax.all_to_all(
        back.reshape(n_exp, CAP, width), ("z", "y"), split_axis=0, concat_axis=0, tiled=True
    )
    grad_gate = (dot_rows(rows_in, r_gate) * scale).astype(BF16)[None]
    grad_up = (dot_rows(rows_in, r_up) * scale).astype(BF16)[None]
    grad_down = (dot_rows(r_act, rows_grad) * scale).astype(BF16)[None]

    rows = jnp.arange(n_rows, dtype=jnp.int32)[:, None]
    spread = (rows // CAP == experts[:, 0][None, :]).astype(BF16)
    placed = (dot(spread, rank.astype(BF16)).astype(jnp.int32) == rows % CAP).astype(BF16)
    routed = dot_rows(placed, back_rows.reshape(n_rows, width))
    grad_tokens = (mine + routed).astype(BF16)
    return (grad_tokens, grad_gate, grad_up, grad_down, own[0].T, own[1].T, own[2])


def solution(mesh):
    n_dp, n_expert = mesh.devices.shape
    fine = Mesh(mesh.devices.reshape(n_dp // 2, 2, n_expert // NY, NY), ("x", "core", "z", "y"))
    dp, ex = ("x", "core"), ("z", "y")
    in_specs = (
        P(ex, dp), P(ex, dp), P(ex, None), P(ex, None), P(ex, dp, None), P(ex, dp, None), P(ex, None, dp),
        P(dp, ex), P(dp, ex), P(ex, dp),
    )
    out_specs = (P(ex, dp), P(ex, dp, None), P(ex, dp, None), P(ex, None, dp), P(dp, ex), P(dp, ex), P(ex, dp))
    return jax.shard_map(shards, mesh=fine, in_specs=in_specs, out_specs=out_specs, check_vma=False)
```

profile of v0, /device:TPU:8, one launch (start us, length us, event | category | flops | bytes accessed | tf_op | source)
XLA Modules:
  0.0 227.3 jit_solution(346706416483291079)
XLA Ops:
  7.3 2.2 pad_maximum_fusion
  17.3 14.5 %collective-permute-done = bf16[2,256,896]{2,1,0:T(8,128)(2,1)S(1)} collective-permute-done((bf16[2,256,896]{2,1,0:T(8,128)(2,1)}, bf16[2,256,896]{2,1,0:T(8,128)(2,1)S(1)}, u32[]{:S(2)}, u32[]{:S(2)}) %collective-permute-start) | collective-permute-done | bytes 917536 | tf_op jit(solution)/shard_map/ppermute | solution.py:42
  34.0 11.4 %all-to-all-start = ((bf16[32,24,896]{2,1,0:T(8,128)(2,1)}), bf16[32,24,896]{2,1,0:T(8,128)(2,1)S(1)}, u32[]{:S(2)}, u32[]{:S(2)}) async-start(bf16[32,24,896]{2,1,0:T(8,128)(2,1)} %multiply_convert_fusion.3), calls=%async_computation | async-start | bytes 2752512 | tf_op jit(solution)/shard_map/all_to_all | solution.py:285
  47.1 1.8 collective-permute-start.2
  49.1 15.9 %collective-permute-done.2 = bf16[2,128,896]{2,1,0:T(8,128)(2,1)S(1)} collective-permute-done((bf16[2,128,896]{2,1,0:T(8,128)(2,1)S(1)}, bf16[2,128,896]{2,1,0:T(8,128)(2,1)S(1)}, u32[]{:S(2)}, u32[]{:S(2)}) %collective-permute-start.2) | collective-permute-done | bytes 458784 | tf_op jit(solution)/shard_map/ppermute | solution.py:42
  65.1 1.8 copy-done
  66.9 2.0 copy-done.1
  70.3 3.2 %shared_partials.1 = (bf16[512,768]{1,0:T(8,128)(2,1)S(1)}, f32[512,768]{1,0:T(8,128)S(1)}) custom-call(s32[2]{0:T(128)S(1)} %pad_add_fusion.where, bf16[4,2,256,896]{3,2,1,0:T(8,128)(2,1)S(1)} %copy-done.1, bf16[4,2,256,896]{3,2,1,0:T(8,128)(2,1)S(1)} %copy-done.1, bf16[8,96,896]{2,1,0:T(8,128)(2,1)S(1)} %bitcast.110), custom_call_target="tpu_custom_call" | custom-call | flops 1409286144 | bytes 3670016 | tf_op jit(solution)/shard_map/shared_partials/pallas_call | solution.py:115
  74.9 5.9 %all-to-all-done = bf16[32,24,896]{2,1,0:T(8,128)(2,1)S(1)} async-done(((bf16[32,24,896]{2,1,0:T(8,128)(2,1)}), bf16[32,24,896]{2,1,0:T(8,128)(2,1)S(1)}, u32[]{:S(2)}, u32[]{:S(2)}) %all-to-all-start) | async-done | bytes 1376288 | tf_op jit(solution)/shard_map/all_to_all | solution.py:285
  85.3 6.6 %routed_partials.1 = (bf16[768,896]{1,0:T(8,128)(2,1)S(1)}, bf16[192,3072]{1,0:T(8,128)(2,1)}, f32[192,3072]{1,0:T(8,128)S(1)}) custom-call(s32[2]{0:T(128)S(1)} %pad_add_fusion.where, bf16[768,768]{1,0:T(8,128)(2,1)S(1)} %fusion.compact, bf16[768,896]{1,0:T(8,128)(2,1)S(1)} %bitcast.112, bf16[1,896,1024]{2,1,0:T(8,128)(2,1)S(1)} %copy-done.10, ...), custom_call_target="tpu_custom_call" | custom-call | flops 2113929216 | bytes 5505024 | tf_op jit(solution)/shard_map/routed_partials/pallas_call | solution.py:224
  94.4 1.9 convert_add_fusion.1
  99.8 1.8 collective-permute-start.7
  101.6 1.8 collective-permute-start.6
  103.4 3.8 %collective-permute-done.5 = bf16[128,768]{1,0:T(8,128)(2,1)} collective-permute-done((bf16[128,768]{1,0:T(8,128)(2,1)}, bf16[128,768]{1,0:T(8,128)(2,1)}, u32[]{:S(2)}, u32[]{:S(2)}) %collective-permute-start.5) | collective-permute-done | bytes 196640 | tf_op jit(solution)/shard_map/ppermute | solution.py:42
  107.2 3.5 %collective-permute-done.7 = bf16[128,768]{1,0:T(8,128)(2,1)} collective-permute-done((bf16[128,768]{1,0:T(8,128)(2,1)}, bf16[128,768]{1,0:T(8,128)(2,1)}, u32[]{:S(2)}, u32[]{:S(2)}) %collective-permute-start.7) | collective-permute-done | bytes 196640 | tf_op jit(solution)/shard_map/ppermute | solution.py:42
  115.1 2.1 collective-permute-start.16
  117.2 2.4 %collective-permute-start.17 = (bf16[48,3072]{1,0:T(8,128)(2,1)S(1)}, bf16[48,3072]{1,0:T(8,128)(2,1)S(1)}, u32[]{:S(2)}, u32[]{:S(2)}) collective-permute-start(bf16[48,3072]{1,0:T(8,128)(2,1)S(1)} %get-tuple-element.37), channel_id=1, source_target_pairs={{0,128},{64,192},{128,0},{192,64},{1,129},{65,193},{129,1},{193,65... | collective-permute-start | bytes 884744 | tf_op jit(solution)/shard_map/ppermute | solution.py:42
  121.6 2.0 collective-permute-done.10.refs_2_
  123.6 2.1 collective-permute-start.9
  125.8 13.4 %collective-permute-done.11.refs_3_ = bf16[128,768]{1,0:T(8,128)(2,1)S(1)} collective-permute-done((bf16[128,768]{1,0:T(8,128)(2,1)S(1)}, bf16[128,768]{1,0:T(8,128)(2,1)S(1)}, u32[]{:S(2)}, u32[]{:S(2)}) %collective-permute-start.11) | collective-permute-done | bytes 196640 | tf_op jit(solution)/shard_map/ppermute | solution.py:42
  142.7 6.8 %shared_back.1 = (f32[256,896]{1,0:T(8,128)S(1)}, bf16[4,256,896]{2,1,0:T(8,128)(2,1)S(1)}, f32[8,96,896]{2,1,0:T(8,128)}) custom-call(bf16[1024,768]{1,0:T(8,128)(2,1)S(1)} %bitcast.109, bf16[4,2,256,896]{3,2,1,0:T(8,128)(2,1)S(1)} %copy-done.2, bf16[4,2,256,896]{3,2,1,0:T(8,128)(2,1)S(1)} %copy-done.2, bf16[8,96,896]{2,1,0:T(8,128)(2,1)S(1)} %bitcast.111), custom_call_target="tpu_custom_call" | custom-call | flops 2348810240 | bytes 7340032 | tf_op jit(solution)/shard_map/shared_back/pallas_call | solution.py:169
  153.9 1.9 collective-permute-start.20
  155.8 2.8 %collective-permute-start.23 = (bf16[48,3072]{1,0:T(8,128)(2,1)S(1)}, bf16[48,3072]{1,0:T(8,128)(2,1)S(1)}, u32[]{:S(2)}, u32[]{:S(2)}) collective-permute-start(bf16[48,3072]{1,0:T(8,128)(2,1)S(1)} %pad_maximum_fusion.1.refs_0_), channel_id=1, source_target_pairs={{0,192},{64,0},{128,64},{192,128},{1,193},{65,1},{129,65},{193,129... | collective-permute-start | bytes 884744 | tf_op jit(solution)/shard_map/ppermute | solution.py:42
  158.6 2.1 collective-permute-done.24.refs_3_
  160.9 9.5 %collective-permute-done.23.refs_1_ = bf16[48,3072]{1,0:T(8,128)(2,1)S(1)} collective-permute-done((bf16[48,3072]{1,0:T(8,128)(2,1)S(1)}, bf16[48,3072]{1,0:T(8,128)(2,1)S(1)}, u32[]{:S(2)}, u32[]{:S(2)}) %collective-permute-start.23) | collective-permute-done | bytes 294944 | tf_op jit(solution)/shard_map/ppermute | solution.py:42
  171.8 4.0 %collective-permute-done.20 = bf16[256,896]{1,0:T(8,128)(2,1)S(1)} collective-permute-done((bf16[256,896]{1,0:T(8,128)(2,1)S(1)}, bf16[256,896]{1,0:T(8,128)(2,1)S(1)}, u32[]{:S(2)}, u32[]{:S(2)}) %collective-permute-start.20) | collective-permute-done | bytes 458784 | tf_op jit(solution)/shard_map/ppermute | solution.py:42
  181.7 7.2 %all-to-all-start.1 = ((bf16[32,12,896]{2,1,0:T(8,128)(2,1)}), bf16[32,12,896]{2,1,0:T(8,128)(2,1)}, u32[]{:S(2)}, u32[]{:S(2)}) async-start(bf16[32,12,896]{2,1,0:T(8,128)(2,1)} %reshape.567), calls=%async_computation.1 | async-start | bytes 1835008 | tf_op jit(solution)/shard_map/all_to_all | solution.py:329
  189.0 3.6 %fusion.5 = bf16[1,896,1024]{2,1,0:T(8,128)(2,1)} fusion(bf16[384,3072]{1,0:T(8,128)(2,1)S(1)} %bitcast.115, bf16[768,896]{1,0:T(8,128)(2,1)} %copy-done.15), kind=kOutput, calls=%fused_computation.13 | convolution fusion | flops 706478080 | bytes 3309568 | tf_op jit(solution)/shard_map/dot_general | solution.py:21
  192.6 2.4 %fusion.6 = bf16[1,896,1024]{2,1,0:T(8,128)(2,1)} fusion(bf16[384,3072]{1,0:T(8,128)(2,1)S(1)} %bitcast.116, bf16[768,896]{1,0:T(8,128)(2,1)S(1)} %copy-done.16), kind=kOutput, calls=%fused_computation.14 | convolution fusion | flops 706478080 | bytes 3309568 | tf_op jit(solution)/shard_map/dot_general | solution.py:21
  195.0 2.5 %fusion.7 = bf16[1,1024,896]{2,1,0:T(8,128)(2,1)} fusion(bf16[384,3072]{1,0:T(8,128)(2,1)S(1)} %bitcast.117, bf16[768,896]{1,0:T(8,128)(2,1)S(1)} %copy-done.16), kind=kOutput, calls=%fused_computation.15 | convolution fusion | flops 706478080 | bytes 3309568 | tf_op jit(solution)/shard_map/dot_general | solution.py:21
  197.5 17.1 %all-to-all-done.1 = bf16[32,12,896]{2,1,0:T(8,128)(2,1)} async-done(((bf16[32,12,896]{2,1,0:T(8,128)(2,1)}), bf16[32,12,896]{2,1,0:T(8,128)(2,1)}, u32[]{:S(2)}, u32[]{:S(2)}) %all-to-all-start.1) | async-done | bytes 688160 | tf_op jit(solution)/shard_map/all_to_all | solution.py:329
  216.6 2.1 add_convert_fusion
  (159 shorter events, 50.6 us)
Async XLA Ops:
  7.2 59.7 %all-gather.2.cloned.1.call-start = ((), (), s32[]{:S(2)}) async-start(), calls=%async_computation.3 | async-start | bytes 1548288 | tf_op jit(solution)/shard_map/all_gather | solution.py:258
  9.5 22.3 %collective-permute-start = (bf16[2,256,896]{2,1,0:T(8,128)(2,1)}, bf16[2,256,896]{2,1,0:T(8,128)(2,1)S(1)}, u32[]{:S(2)}, u32[]{:S(2)}) collective-permute-start(bf16[2,256,896]{2,1,0:T(8,128)(2,1)} %get-tuple-element.58), channel_id=1, source_target_pairs={{0,1},{1,2},{2,3},{3,0},{4,5},{5,6},{6,7},{7,4},{8,9},{9,10},{10,1... | collective-permute-start | bytes 2752520 | tf_op jit(solution)/shard_map/ppermute | solution.py:42
  11.1 22.0 %collective-permute-start.1 = (bf16[2,256,896]{2,1,0:T(8,128)(2,1)}, bf16[2,256,896]{2,1,0:T(8,128)(2,1)S(1)}, u32[]{:S(2)}, u32[]{:S(2)}) collective-permute-start(bf16[2,256,896]{2,1,0:T(8,128)(2,1)} %get-tuple-element.58), channel_id=1, source_target_pairs={{0,3},{1,0},{2,1},{3,2},{4,7},{5,4},{6,5},{7,6},{8,11},{9,8},{10,9... | collective-permute-start | bytes 2752520 | tf_op jit(solution)/shard_map/ppermute | solution.py:42
  34.0 46.8 %all-to-all-start = ((bf16[32,24,896]{2,1,0:T(8,128)(2,1)}), bf16[32,24,896]{2,1,0:T(8,128)(2,1)S(1)}, u32[]{:S(2)}, u32[]{:S(2)}) async-start(bf16[32,24,896]{2,1,0:T(8,128)(2,1)} %multiply_convert_fusion.3), calls=%async_computation | async-start | bytes 2752512 | tf_op jit(solution)/shard_map/all_to_all | solution.py:285
  45.5 173.2 %reduce-scatter.2.cloned.1.call-start = ((), (), s32[]{:S(2)}) async-start(), calls=%async_computation.4 | async-start | bytes 3096576 | tf_op jit(solution)/shard_map/reduce_scatter | solution.py:323
  46.7 18.3 %collective-permute-start.3 = (bf16[2,128,896]{2,1,0:T(8,128)(2,1)S(1)}, bf16[2,128,896]{2,1,0:T(8,128)(2,1)S(1)}, u32[]{:S(2)}, u32[]{:S(2)}) collective-permute-start(bf16[2,128,896]{2,1,0:T(8,128)(2,1)S(1)} %slice.125), channel_id=1, source_target_pairs={{0,3},{1,0},{2,1},{3,2},{4,7},{5,4},{6,5},{7,6},{8,11},{9,8},{10,9... | collective-permute-start | bytes 1376264 | tf_op jit(solution)/shard_map/ppermute | solution.py:42
  47.1 18.0 %collective-permute-start.2 = (bf16[2,128,896]{2,1,0:T(8,128)(2,1)S(1)}, bf16[2,128,896]{2,1,0:T(8,128)(2,1)S(1)}, u32[]{:S(2)}, u32[]{:S(2)}) collective-permute-start(bf16[2,128,896]{2,1,0:T(8,128)(2,1)S(1)} %slice.124), channel_id=1, source_target_pairs={{0,1},{1,2},{2,3},{3,0},{4,5},{5,6},{6,7},{7,4},{8,9},{9,10},{10,1... | collective-permute-start | bytes 1376264 | tf_op jit(solution)/shard_map/ppermute | solution.py:42
  74.6 19.8 %collective-permute-start.4 = (bf16[512,768]{1,0:T(8,128)(2,1)S(1)}, bf16[512,768]{1,0:T(8,128)(2,1)}, u32[]{:S(2)}, u32[]{:S(2)}) collective-permute-start(bf16[512,768]{1,0:T(8,128)(2,1)S(1)} %get-tuple-element.31), channel_id=1, source_target_pairs={{0,32},{32,0},{1,33},{33,1},{2,34},{34,2},{3,35},{35,3},{4,36},{36... | collective-permute-start | bytes 2359304 | tf_op jit(solution)/shard_map/ppermute | solution.py:42
  94.4 19.3 %collective-permute-start.8 = (bf16[192,3072]{1,0:T(8,128)(2,1)}, bf16[192,3072]{1,0:T(8,128)(2,1)S(1)}, u32[]{:S(2)}, u32[]{:S(2)}) collective-permute-start(bf16[192,3072]{1,0:T(8,128)(2,1)} %get-tuple-element.34), channel_id=1, source_target_pairs={{0,32},{32,0},{1,33},{33,1},{2,34},{34,2},{3,35},{35,3},{4,36},{36... | collective-permute-start | bytes 3538952 | tf_op jit(solution)/shard_map/ppermute | solution.py:42
  98.4 8.8 %collective-permute-start.5 = (bf16[128,768]{1,0:T(8,128)(2,1)}, bf16[128,768]{1,0:T(8,128)(2,1)}, u32[]{:S(2)}, u32[]{:S(2)}) collective-permute-start(bf16[128,768]{1,0:T(8,128)(2,1)} %get-tuple-element.55), channel_id=1, source_target_pairs={{0,64},{64,128},{128,192},{192,0},{1,65},{65,129},{129,193},{193,1... | collective-permute-start | bytes 589832 | tf_op jit(solution)/shard_map/ppermute | solution.py:42
  99.8 10.9 %collective-permute-start.7 = (bf16[128,768]{1,0:T(8,128)(2,1)}, bf16[128,768]{1,0:T(8,128)(2,1)}, u32[]{:S(2)}, u32[]{:S(2)}) collective-permute-start(bf16[128,768]{1,0:T(8,128)(2,1)} %get-tuple-element.56), channel_id=1, source_target_pairs={{0,192},{64,0},{128,64},{192,128},{1,193},{65,1},{129,65},{193,129... | collective-permute-start | bytes 589832 | tf_op jit(solution)/shard_map/ppermute | solution.py:42
  101.6 10.7 %collective-permute-start.6 = (bf16[128,768]{1,0:T(8,128)(2,1)}, bf16[128,768]{1,0:T(8,128)(2,1)}, u32[]{:S(2)}, u32[]{:S(2)}) collective-permute-start(bf16[128,768]{1,0:T(8,128)(2,1)} %get-tuple-element.57), channel_id=1, source_target_pairs={{0,128},{64,192},{128,0},{192,64},{1,129},{65,193},{129,1},{193,65... | collective-permute-start | bytes 589832 | tf_op jit(solution)/shard_map/ppermute | solution.py:42
  114.2 9.4 %collective-permute-start.10 = (bf16[128,768]{1,0:T(8,128)(2,1)S(1)}, bf16[128,768]{1,0:T(8,128)(2,1)S(1)}, u32[]{:S(2)}, u32[]{:S(2)}) collective-permute-start(bf16[128,768]{1,0:T(8,128)(2,1)S(1)} %pad_maximum_fusion.2.refs_0_), channel_id=1, source_target_pairs={{0,128},{64,192},{128,0},{192,64},{1,129},{65,193},{129,1},{193,65... | collective-permute-start | bytes 589832 | tf_op jit(solution)/shard_map/ppermute | solution.py:42
  115.1 24.6 %collective-permute-start.16 = (bf16[48,3072]{1,0:T(8,128)(2,1)S(1)}, bf16[48,3072]{1,0:T(8,128)(2,1)S(1)}, u32[]{:S(2)}, u32[]{:S(2)}) collective-permute-start(bf16[48,3072]{1,0:T(8,128)(2,1)S(1)} %get-tuple-element.36), channel_id=1, source_target_pairs={{0,64},{64,128},{128,192},{192,0},{1,65},{65,129},{129,193},{193,1... | collective-permute-start | bytes 884744 | tf_op jit(solution)/shard_map/ppermute | solution.py:42
  117.2 22.6 %collective-permute-start.17 = (bf16[48,3072]{1,0:T(8,128)(2,1)S(1)}, bf16[48,3072]{1,0:T(8,128)(2,1)S(1)}, u32[]{:S(2)}, u32[]{:S(2)}) collective-permute-start(bf16[48,3072]{1,0:T(8,128)(2,1)S(1)} %get-tuple-element.37), channel_id=1, source_target_pairs={{0,128},{64,192},{128,0},{192,64},{1,129},{65,193},{129,1},{193,65... | collective-permute-start | bytes 884744 | tf_op jit(solution)/shard_map/ppermute | solution.py:42
  119.6 20.6 %collective-permute-start.18 = (bf16[48,3072]{1,0:T(8,128)(2,1)S(1)}, bf16[48,3072]{1,0:T(8,128)(2,1)S(1)}, u32[]{:S(2)}, u32[]{:S(2)}) collective-permute-start(bf16[48,3072]{1,0:T(8,128)(2,1)S(1)} %get-tuple-element.38), channel_id=1, source_target_pairs={{0,192},{64,0},{128,64},{192,128},{1,193},{65,1},{129,65},{193,129... | collective-permute-start | bytes 884744 | tf_op jit(solution)/shard_map/ppermute | solution.py:42
  120.4 18.7 %collective-permute-start.11 = (bf16[128,768]{1,0:T(8,128)(2,1)S(1)}, bf16[128,768]{1,0:T(8,128)(2,1)S(1)}, u32[]{:S(2)}, u32[]{:S(2)}) collective-permute-start(bf16[128,768]{1,0:T(8,128)(2,1)S(1)} %pad_maximum_fusion.2.refs_0_), channel_id=1, source_target_pairs={{0,64},{64,128},{128,192},{192,0},{1,65},{65,129},{129,193},{193,1... | collective-permute-start | bytes 589832 | tf_op jit(solution)/shard_map/ppermute | solution.py:42
  123.6 15.6 %collective-permute-start.9 = (bf16[128,768]{1,0:T(8,128)(2,1)S(1)}, bf16[128,768]{1,0:T(8,128)(2,1)S(1)}, u32[]{:S(2)}, u32[]{:S(2)}) collective-permute-start(bf16[128,768]{1,0:T(8,128)(2,1)S(1)} %pad_maximum_fusion.2.refs_0_), channel_id=1, source_target_pairs={{0,192},{64,0},{128,64},{192,128},{1,193},{65,1},{129,65},{193,129... | collective-permute-start | bytes 589832 | tf_op jit(solution)/shard_map/ppermute | solution.py:42
  139.2 2.0 collective-permute-start.14
  139.7 1.5 collective-permute-start.15
  139.8 1.7 collective-permute-start.13
  150.4 10.3 %collective-permute-start.24 = (bf16[48,3072]{1,0:T(8,128)(2,1)S(1)}, bf16[48,3072]{1,0:T(8,128)(2,1)S(1)}, u32[]{:S(2)}, u32[]{:S(2)}) collective-permute-start(bf16[48,3072]{1,0:T(8,128)(2,1)S(1)} %pad_maximum_fusion.1.refs_0_), channel_id=1, source_target_pairs={{0,64},{64,128},{128,192},{192,0},{1,65},{65,129},{129,193},{193,1... | collective-permute-start | bytes 884744 | tf_op jit(solution)/shard_map/ppermute | solution.py:42
  151.0 19.9 %collective-permute-start.22 = (bf16[256,896]{1,0:T(8,128)(2,1)S(1)}, bf16[256,896]{1,0:T(8,128)(2,1)}, u32[]{:S(2)}, u32[]{:S(2)}) collective-permute-start(bf16[256,896]{1,0:T(8,128)(2,1)S(1)} %get-tuple-element.52), channel_id=1, source_target_pairs={{0,1},{1,2},{2,3},{3,0},{4,5},{5,6},{6,7},{7,4},{8,9},{9,10},{10,1... | collective-permute-start | bytes 1376264 | tf_op jit(solution)/shard_map/ppermute | solution.py:42
  152.5 18.5 %collective-permute-start.21 = (bf16[256,896]{1,0:T(8,128)(2,1)S(1)}, bf16[256,896]{1,0:T(8,128)(2,1)S(1)}, u32[]{:S(2)}, u32[]{:S(2)}) collective-permute-start(bf16[256,896]{1,0:T(8,128)(2,1)S(1)} %get-tuple-element.53), channel_id=1, source_target_pairs={{0,2},{1,3},{2,0},{3,1},{4,6},{5,7},{6,4},{7,5},{8,10},{9,11},{10,... | collective-permute-start | bytes 1376264 | tf_op jit(solution)/shard_map/ppermute | solution.py:42
  153.9 21.8 %collective-permute-start.20 = (bf16[256,896]{1,0:T(8,128)(2,1)S(1)}, bf16[256,896]{1,0:T(8,128)(2,1)S(1)}, u32[]{:S(2)}, u32[]{:S(2)}) collective-permute-start(bf16[256,896]{1,0:T(8,128)(2,1)S(1)} %get-tuple-element.54), channel_id=1, source_target_pairs={{0,3},{1,0},{2,1},{3,2},{4,7},{5,4},{6,5},{7,6},{8,11},{9,8},{10,9... | collective-permute-start | bytes 1376264 | tf_op jit(solution)/shard_map/ppermute | solution.py:42
  155.8 14.6 %collective-permute-start.23 = (bf16[48,3072]{1,0:T(8,128)(2,1)S(1)}, bf16[48,3072]{1,0:T(8,128)(2,1)S(1)}, u32[]{:S(2)}, u32[]{:S(2)}) collective-permute-start(bf16[48,3072]{1,0:T(8,128)(2,1)S(1)} %pad_maximum_fusion.1.refs_0_), channel_id=1, source_target_pairs={{0,192},{64,0},{128,64},{192,128},{1,193},{65,1},{129,65},{193,129... | collective-permute-start | bytes 884744 | tf_op jit(solution)/shard_map/ppermute | solution.py:42
  160.7 9.7 %collective-permute-start.19 = (bf16[48,3072]{1,0:T(8,128)(2,1)S(1)}, bf16[48,3072]{1,0:T(8,128)(2,1)S(1)}, u32[]{:S(2)}, u32[]{:S(2)}) collective-permute-start(bf16[48,3072]{1,0:T(8,128)(2,1)S(1)} %pad_maximum_fusion.1.refs_0_), channel_id=1, source_target_pairs={{0,128},{64,192},{128,0},{192,64},{1,129},{65,193},{129,1},{193,65... | collective-permute-start | bytes 884744 | tf_op jit(solution)/shard_map/ppermute | solution.py:42
  170.4 5.4 %collective-permute-start.25 = (bf16[48,3072]{1,0:T(8,128)(2,1)S(1)}, bf16[48,3072]{1,0:T(8,128)(2,1)S(1)}, u32[]{:S(2)}, u32[]{:S(2)}) collective-permute-start(bf16[48,3072]{1,0:T(8,128)(2,1)S(1)} %pad_maximum_fusion.1.refs_0_), channel_id=1, source_target_pairs={{0,32},{32,0},{1,33},{33,1},{2,34},{34,2},{3,35},{35,3},{4,36},{36... | collective-permute-start | bytes 884744 | tf_op jit(solution)/shard_map/ppermute | solution.py:42
  170.4 5.4 %collective-permute-start.28 = (bf16[48,3072]{1,0:T(8,128)(2,1)S(1)}, bf16[48,3072]{1,0:T(8,128)(2,1)S(1)}, u32[]{:S(2)}, u32[]{:S(2)}) collective-permute-start(bf16[48,3072]{1,0:T(8,128)(2,1)S(1)} %collective-permute-done.24.refs_3_), channel_id=1, source_target_pairs={{0,32},{32,0},{1,33},{33,1},{2,34},{34,2},{3,35},{35,3},{4,36},{36... | collective-permute-start | bytes 884744 | tf_op jit(solution)/shard_map/ppermute | solution.py:42
  170.9 4.9 %collective-permute-start.26 = (bf16[48,3072]{1,0:T(8,128)(2,1)S(1)}, bf16[48,3072]{1,0:T(8,128)(2,1)S(1)}, u32[]{:S(2)}, u32[]{:S(2)}) collective-permute-start(bf16[48,3072]{1,0:T(8,128)(2,1)S(1)} %collective-permute-done.23.refs_1_), channel_id=1, source_target_pairs={{0,32},{32,0},{1,33},{33,1},{2,34},{34,2},{3,35},{35,3},{4,36},{36... | collective-permute-start | bytes 884744 | tf_op jit(solution)/shard_map/ppermute | solution.py:42
  175.8 1.6 collective-permute-start.27
  181.7 32.9 %all-to-all-start.1 = ((bf16[32,12,896]{2,1,0:T(8,128)(2,1)}), bf16[32,12,896]{2,1,0:T(8,128)(2,1)}, u32[]{:S(2)}, u32[]{:S(2)}) async-start(bf16[32,12,896]{2,1,0:T(8,128)(2,1)} %reshape.567), calls=%async_computation.1 | async-start | bytes 1835008 | tf_op jit(solution)/shard_map/all_to_all | solution.py:329
  (33 other events, 184.1 us)
Sparse Core Ops, SparseCore 0:
  12.5 46.4 all-gather.1
  150.5 40.4 reduce-scatter.1
where the time goes:
time: 228 us; the launch traced here: 227 us
  waiting for transfers between devices  97.2 us (43%)
  starting transfers between devices  47.5 us (21%)
  local copies, waits for them, and re-layouts  25.2 us (11%)
  Pallas kernels  17.9 us (8%)
  between operations  14.6 us (6%)
  matrix products  13.6 us (6%)
  other arithmetic  11.4 us (5%)
    ppermute x29, waiting for transfers between devices, shift(): lax.ppermute(value, axis, [(i, (i + by) % size) for i in range(size)])  74.1 us
    ppermute x29, starting transfers between devices, shift(): lax.ppermute(value, axis, [(i, (i + by) % size) for i in range(size)])  28.7 us
    unnamed x64, local copies, waits for them, and re-layouts  18.9 us
    all_to_all x1, waiting for transfers between devices, shards(): lax.all_to_all(back.reshape(n_exp, CAP, width), ('z', 'y'), split_axis=0,...  17.1 us
    all_to_all x1, starting transfers between devices, shards(): lax.all_to_all(send, ('z', 'y'), split_axis=0, concat_axis=0, tiled=True)  11.4 us
    dot_general x4, matrix products, dot_rows(): lax.dot_general(left, right, (((0,), (0,)), ((), ())), preferred_element_...  9.17 us
    all_to_all x1, starting transfers between devices, shards(): lax.all_to_all(back.reshape(n_exp, CAP, width), ('z', 'y'), split_axis=0,...  7.25 us
    pallas_call x1, Pallas kernels, shared_back(): pl.pallas_call(lambda *refs: back_kernel(scale, *refs), out_shape=(jax.Sh...  6.77 us
  transfers between devices with their start and end apart: 33, of which 17 were waited for; matrix products, arithmetic and copies ran while one was open for 12% of the time, Pallas kernels for 5%

commit v1 on v0

v1 whole, which is shorter than its diff:
```python
import jax
import jax.numpy as jnp
from jax import lax
from jax.experimental import pallas as pl
from jax.experimental.pallas import tpu as pltpu
from jax.sharding import Mesh
from jax.sharding import PartitionSpec as P

CAP = 12
NY = 4
BF16 = jnp.bfloat16
F32 = jnp.float32


def silu_parts(pre):
    sigmoid_val = jax.nn.sigmoid(pre)
    return (pre * sigmoid_val, sigmoid_val * (1.0 + pre * (1.0 - sigmoid_val)))


def dot_rows(left, right):
    return lax.dot_general(left, right, (((0,), (0,)), ((), ())), preferred_element_type=F32)


def dot_cols(left, right):
    return lax.dot_general(left, right, (((1,), (1,)), ((), ())), preferred_element_type=F32)


def dot(left, right):
    return jnp.dot(left, right, preferred_element_type=F32)


def hidden_products(part_gate, part_up, part_act):
    silu_val, silu_slope = silu_parts(part_gate)
    activated = (silu_val * part_up).astype(BF16)
    grad_gate_pre = (part_act * part_up * silu_slope).astype(BF16)
    grad_up_pre = (part_act * silu_val).astype(BF16)
    return (activated, grad_gate_pre, grad_up_pre)


def shift(value, axis, by):
    size = lax.axis_size(axis)
    return lax.ppermute(value, axis, [(i, (i + by) % size) for i in range(size)])


def pick(value, index, axis):
    return lax.dynamic_index_in_dim(value, index, axis, keepdims=False)


VMEM = pl.BlockSpec(memory_space=pltpu.VMEM)
SMEM = pl.BlockSpec(memory_space=pltpu.SMEM)
SMALL = pltpu.CompilerParams(vmem_limit_bytes=2 << 20)


def piece_kernel(where, kept, got, own, *pieces):
    block = own.shape[0]
    n_x = len(pieces) + 1
    for j in range(n_x):
        rows = pl.ds(pl.multiple_of(((where[0] + j) & (n_x - 1)) * block, block), block)
        summed = kept[rows, :] + got[rows, :].astype(F32)
        if j == 0:
            own[...] = summed
        else:
            pieces[j - 1][...] = summed.astype(BF16)


def x_pieces(where, kept, got):
    n_x = lax.axis_size("x")
    block, cols = kept.shape[0] // n_x, kept.shape[1]
    own, *pieces = pl.pallas_call(
        piece_kernel,
        out_shape=[jax.ShapeDtypeStruct((block, cols), F32)]
        + [jax.ShapeDtypeStruct((block, cols), BF16)] * (n_x - 1),
        in_specs=[SMEM, VMEM, VMEM],
        out_specs=[VMEM] * n_x,
        compiler_params=SMALL,
        cost_estimate=pl.CostEstimate(flops=n_x * block * cols, bytes_accessed=8 * n_x * block * cols, transcendentals=0),
        name="x_pieces",
    )(where, kept, got)
    return own, pieces


def act_kernel(own, *refs):
    *got, out = refs
    cols = own.shape[1] // 3
    sums = []
    for k in range(3):
        spot = slice(k * cols, (k + 1) * cols)
        total = own[:, spot].astype(F32)
        for piece in got:
            total = total + piece[:, spot].astype(F32)
        sums.append(total)
    for k, value in enumerate(hidden_products(*sums)):
        out[:, k * cols : (k + 1) * cols] = value


def x_exchange(pieces):
    return [shift(piece, "x", j + 1) for j, piece in enumerate(pieces)]


def x_products(own, got):
    return pl.pallas_call(
        act_kernel,
        out_shape=jax.ShapeDtypeStruct(own.shape, BF16),
        in_specs=[VMEM] * (1 + len(got)),
        out_specs=VMEM,
        compiler_params=SMALL,
        cost_estimate=pl.CostEstimate(flops=10 * own.size, bytes_accessed=12 * own.size, transcendentals=own.size),
        name="x_products",
    )(own, *got)


def x_blocks(value):
    return [value] + [shift(value, "x", -j) for j in range(1, lax.axis_size("x"))]


def both_cores(blocks):
    return blocks + [shift(block, "core", 1) for block in blocks]


def place_kernel(where, *refs):
    *blocks, out = refs
    n_core, n_x = out.shape[:2]
    for i, block in enumerate(blocks):
        out[(where[1] + i // n_x) & (n_core - 1), (where[0] + i % n_x) & (n_x - 1)] = block[...]


def place_blocks(blocks, where):
    n_x = lax.axis_size("x")
    rows, cols = blocks[0].shape
    out = pl.pallas_call(
        place_kernel,
        out_shape=jax.ShapeDtypeStruct((2, n_x, rows, cols), blocks[0].dtype),
        in_specs=[pl.BlockSpec(memory_space=pltpu.SMEM)] + [pl.BlockSpec(memory_space=pltpu.VMEM)] * len(blocks),
        out_specs=pl.BlockSpec(memory_space=pltpu.VMEM),
        compiler_params=pltpu.CompilerParams(vmem_limit_bytes=2 << 20),
        cost_estimate=pl.CostEstimate(flops=0, bytes_accessed=8 * n_x * rows * cols, transcendentals=0),
        name="place_blocks",
    )(where, *blocks)
    return out.reshape(2 * n_x * rows, cols)


def part_kernel(where, tok, grd, weights, send, kept):
    step = pl.program_id(0)
    units = weights.shape[1] // 3
    width = weights.shape[2]
    sh = weights.shape[0] * units
    gate, up, down = (weights[:, k * units : (k + 1) * units].reshape(sh, width) for k in range(3))
    n_tok = tok.shape[1]
    part = [dot_cols(tok[0], gate), dot_cols(tok[0], up), dot_cols(grd[0], down)]

    @pl.when(step < 2)
    def _():
        for k in range(3):
            send[pl.ds(pl.multiple_of(step * n_tok, n_tok), n_tok), k * sh : (k + 1) * sh] = part[k].astype(BF16)

    @pl.when(step >= 2)
    def _():
        for k in range(3):
            kept[pl.ds(pl.multiple_of((step - 2) * n_tok, n_tok), n_tok), k * sh : (k + 1) * sh] = part[k]


def shared_partials(where, tok, grd, weights):
    n_y, n_tok, width = tok.shape
    cols = weights.shape[0] * weights.shape[1]
    rows = pl.BlockSpec((1, n_tok, width), lambda i, where: ((i + 2 * (1 - where[1])) & 3, 0, 0))
    return pl.pallas_call(
        part_kernel,
        out_shape=(
            jax.ShapeDtypeStruct((2 * n_tok, cols), BF16),
            jax.ShapeDtypeStruct((2 * n_tok, cols), F32),
        ),
        grid_spec=pltpu.PrefetchScalarGridSpec(
            num_scalar_prefetch=1,
            grid=(n_y,),
            in_specs=[rows, rows, pl.BlockSpec(weights.shape, lambda i, where: (0, 0, 0), pipeline_mode=pl.Buffered(1))],
            out_specs=[VMEM, VMEM],
        ),
        compiler_params=pltpu.CompilerParams(vmem_limit_bytes=11 << 20),
        cost_estimate=pl.CostEstimate(
            flops=2 * n_y * n_tok * width * cols, bytes_accessed=4 * n_y * n_tok * width, transcendentals=0
        ),
        name="shared_partials",
    )(where, *(pltpu.with_memory_space_constraint(v, pltpu.HBM) for v in (tok, grd, weights)))


def back_kernel(scale, products, tok, grd, weights, mine, back, own, total_own):
    step = pl.program_id(0)
    nz, units, width = weights.shape[0], weights.shape[1] // 3, weights.shape[2]
    sh = nz * units
    gate, up = (weights[:, k * units : (k + 1) * units].reshape(sh, width) for k in range(2))
    n_tok = tok.shape[1]
    spot = pl.ds(pl.multiple_of(step * n_tok, n_tok), n_tok)
    act, d_gate, d_up = (products[spot, k * sh : (k + 1) * sh] for k in range(3))
    total = dot(d_gate, gate) + dot(d_up, up)
    back[step] = total.astype(BF16)

    @pl.when(step == 0)
    def _():
        mine[...] = total

    grads = [dot_rows(d_gate, tok[0]), dot_rows(d_up, tok[0]), dot_rows(act, grd[0])]

    @pl.when(step == 0)
    def _():
        for k in range(3):
            total_own[:, k * units : (k + 1) * units] = (grads[k] * scale).reshape(nz, units, width)

    @pl.when(step > 0)
    def _():
        for k in range(3):
            total_own[:, k * units : (k + 1) * units] += (grads[k] * scale).reshape(nz, units, width)

    @pl.when(step == pl.num_programs(0) - 1)
    def _():
        own[...] = total_own[...].astype(BF16)


def shared_back(products, tok, grd, weights, scale):
    n_y, n_tok, width = tok.shape
    rows = pl.BlockSpec((1, n_tok, width), lambda i: (i, 0, 0))
    whole = pl.BlockSpec(weights.shape, lambda i: (0, 0, 0), pipeline_mode=pl.Buffered(1))
    cols = products.shape[1]
    return pl.pallas_call(
        lambda *refs: back_kernel(scale, *refs),
        out_shape=(
            jax.ShapeDtypeStruct((n_tok, width), F32),
            jax.ShapeDtypeStruct((n_y, n_tok, width), BF16),
            jax.ShapeDtypeStruct(weights.shape, BF16),
        ),
        grid=(n_y,),
        scratch_shapes=[pltpu.VMEM(weights.shape, F32)],
        in_specs=[VMEM, rows, rows, whole],
        out_specs=[VMEM, VMEM, whole],
        compiler_params=pltpu.CompilerParams(vmem_limit_bytes=16 << 20),
        cost_estimate=pl.CostEstimate(
            flops=10 * n_y * n_tok * width * cols // 3, bytes_accessed=8 * n_y * n_tok * width, transcendentals=0
        ),
        name="shared_back",
    )(products, *(pltpu.with_memory_space_constraint(v, pltpu.HBM) for v in (tok, grd, weights)))


def routed_kernel(where, compact, recv, w_gate, w_up, w_down, rows, send, kept):
    step = pl.program_id(0)
    n_rows, tile = rows.shape[0] // 2, w_gate.shape[2]
    half = n_rows // 2
    hid = send.shape[1] // 3

    @pl.when(step == 0)
    def _():
        rows[...] = dot(compact[...], recv[...]).astype(BF16)

    def ordered(base):
        return jnp.concatenate(
            [
                rows[pl.ds(pl.multiple_of(base + (1 - where[1]) * half, half), half)],
                rows[pl.ds(pl.multiple_of(base + where[1] * half, half), half)],
            ],
            axis=0,
        )

    rows_in, rows_grad = ordered(0), ordered(n_rows)
    part = [dot(rows_in, w_gate[0]), dot(rows_in, w_up[0]), dot_cols(rows_grad, w_down[0])]
    for k in range(3):
        spot = pl.ds(pl.multiple_of(k * hid + step * tile, tile), tile)
        send[:, spot] = part[k][:half].astype(BF16)
        kept[:, spot] = part[k][half:]


def routed_partials(where, compact, recv, w_gate, w_up, w_down):
    n_rows = recv.shape[0] // 2
    width, hid = w_gate.shape[1:]
    tile = min(256, hid)
    out = [
        jax.ShapeDtypeStruct((2 * n_rows, width), BF16),
        jax.ShapeDtypeStruct((n_rows // 2, 3 * hid), BF16),
        jax.ShapeDtypeStruct((n_rows // 2, 3 * hid), F32),
    ]
    return pl.pallas_call(
        routed_kernel,
        out_shape=out,
        grid_spec=pltpu.PrefetchScalarGridSpec(
            num_scalar_prefetch=1,
            grid=(hid // tile,),
            in_specs=[
                VMEM,
                VMEM,
                pl.BlockSpec((1, width, tile), lambda i, where: (0, 0, i)),
                pl.BlockSpec((1, width, tile), lambda i, where: (0, 0, i)),
                pl.BlockSpec((1, tile, width), lambda i, where: (0, i, 0)),
            ],
            out_specs=[VMEM] * 3,
        ),
        compiler_params=pltpu.CompilerParams(vmem_limit_bytes=14 << 20),
        cost_estimate=pl.CostEstimate(
            flops=6 * n_rows * width * hid, bytes_accessed=6 * width * hid, transcendentals=0
        ),
        name="routed_partials",
    )(where, compact, recv, *(pltpu.with_memory_space_constraint(w, pltpu.HBM) for w in (w_gate, w_up, w_down)))


def shards(tokens, grad_out, route_ids, route_gates, w_gate, w_up, w_down, shared_gate, shared_up, shared_down):
    n_z, n_y, n_x = lax.axis_size("z"), lax.axis_size("y"), lax.axis_size("x")
    n_exp = n_z * n_y
    scale = 1.0 / n_exp
    n_tok, width = tokens.shape
    hid = w_gate.shape[2]
    units = shared_down.shape[0]
    sh = n_z * units
    n_rows = n_exp * CAP

    own_w = jnp.concatenate([shared_gate.T, shared_up.T, shared_down], axis=0)

    tokens, grad_out, own_w = lax.optimization_barrier((tokens, grad_out, own_w))
    all_w = lax.all_gather(own_w, "z", axis=0, tiled=True)
    tok_up, tok_down = shift(tokens, "y", 1), shift(tokens, "y", -1)
    grd_up, grd_down = shift(grad_out, "y", 1), shift(grad_out, "y", -1)

    experts = jnp.arange(n_exp, dtype=jnp.int32)[:, None]
    ids, gates = route_ids.T, route_gates.T
    chosen = jnp.zeros((n_exp, n_tok), jnp.bool_)
    gate_total = jnp.zeros((n_exp, n_tok), F32)
    for k in range(ids.shape[0]):
        match = ids[k : k + 1] == experts
        chosen = chosen | match
        gate_total = gate_total + jnp.where(match, gates[k : k + 1], 0.0)
    spots = jnp.arange(n_tok, dtype=jnp.int32)
    earlier = (spots[:, None] < spots[None, :]).astype(BF16)
    rank = dot(chosen.astype(BF16), earlier)
    rank = jnp.where(chosen, rank, -1.0)
    slots = jnp.arange(2 * CAP, dtype=jnp.int32)[None, :, None]
    rank_in = jnp.where(slots < CAP, rank.astype(jnp.int32)[:, None, :], -1) == slots
    rank_grad = jnp.where(slots >= CAP, rank.astype(jnp.int32)[:, None, :] + CAP, -1) == slots
    rank_grad = rank_grad & chosen[:, None, :]
    slot_gate = jnp.sum(jnp.where(rank_grad, gate_total[:, None, :], 0.0), axis=2)
    slot_gate = jnp.where(slots[0, :, 0][None, :] < CAP, 1.0, slot_gate)
    picked = dot(rank_in.astype(BF16).reshape(2 * n_rows, n_tok), tokens)
    picked = picked + dot(rank_grad.astype(BF16).reshape(2 * n_rows, n_tok), grad_out)
    send = (picked.reshape(n_exp, 2 * CAP, width) * slot_gate[:, :, None]).astype(BF16)
    where = jnp.stack([lax.axis_index("x"), lax.axis_index("core")]).astype(jnp.int32)
    spot = jnp.arange(2 * n_rows, dtype=jnp.int32)
    spot = (spot % n_rows) // CAP * (2 * CAP) + spot % CAP + spot // n_rows * CAP
    compact = (spot[:, None] == jnp.arange(2 * n_rows, dtype=jnp.int32)[None, :]).astype(BF16)
    rows = jnp.arange(n_rows, dtype=jnp.int32)[:, None]
    spread = (rows // CAP == experts[:, 0][None, :]).astype(BF16)
    placed = (dot(spread, rank.astype(BF16)).astype(jnp.int32) == rows % CAP).astype(BF16)

    far = n_tok // 2
    tok_beyond = [shift(tok_up[:far], "y", 1), shift(tok_down[far:], "y", -1)]
    grd_beyond = [shift(grd_up[:far], "y", 1), shift(grd_down[far:], "y", -1)]
    send, tok_beyond, where, compact, placed, _ = lax.optimization_barrier(
        (send, tok_beyond, where, compact, placed, own_w)
    )
    recv = lax.all_to_all(send, ("z", "y"), split_axis=0, concat_axis=0, tiled=True)
    groups = []
    for own_rows, up, down, beyond in (
        (tokens, tok_up, tok_down, tok_beyond),
        (grad_out, grd_up, grd_down, grd_beyond),
    ):
        group = jnp.zeros((n_y, n_tok, width), BF16)
        for i, start, part in ((0, 0, own_rows), (1, 0, up), (n_y - 1, 0, down), (2, 0, beyond[0]), (2, far, beyond[1])):
            group = lax.dynamic_update_slice(group, part[None], (i, start, 0))
        groups.append(group)
    group_in, group_grad = groups

    all_w = all_w.reshape(n_z, 3 * units, width)
    s_send, s_kept = shared_partials(where, group_in, group_grad, all_w)
    s_own, s_pieces = x_pieces(where, s_kept, shift(s_send, "core", 1))
    s_mine = x_products(s_own, x_exchange(s_pieces))
    s_products = lax.all_gather(s_mine, ("core", "x"), axis=0, tiled=True)
    recv, _ = lax.optimization_barrier((recv, s_mine))
    rows_all, r_send, r_kept = routed_partials(
        where, compact, recv.reshape(2 * n_rows, width), w_gate, w_up, w_down
    )
    rows_in, rows_grad = rows_all[:n_rows], rows_all[n_rows:]
    r_own, r_pieces = x_pieces(where, r_kept, shift(r_send, "core", 1))

    r_mine = x_products(r_own, x_exchange(r_pieces))
    s_products, r_mine = lax.optimization_barrier((s_products, r_mine))
    mine, s_back, own = shared_back(s_products, group_in, group_grad, all_w, scale)
    r_blocks = x_blocks(r_mine)
    y_got = [shift(s_back[j], "y", -j) for j in range(1, n_y)]
    for got in y_got:
        mine = mine + got.astype(F32)
    own = lax.psum_scatter(own.reshape(n_z * 3 * units, width), "z", scatter_dimension=0, tiled=True)
    own = own.astype(F32).reshape(3, units, width)

    products = place_blocks(both_cores(r_blocks), where)
    r_act, r_gate, r_up = (products[:, k * hid : (k + 1) * hid] for k in range(3))
    back = (dot_cols(r_gate, w_gate[0]) + dot_cols(r_up, w_up[0])).astype(BF16)
    back_rows = lax.all_to_all(
        back.reshape(n_exp, CAP, width), ("z", "y"), split_axis=0, concat_axis=0, tiled=True
    )
    back_rows, *own = lax.optimization_barrier((back_rows, own[0].T, own[1].T, own[2]))
    products, _ = lax.optimization_barrier((products, y_got))
    r_act, r_gate, r_up = (products[:, k * hid : (k + 1) * hid] for k in range(3))
    grad_gate = (dot_rows(rows_in, r_gate) * scale).astype(BF16)[None]
    grad_up = (dot_rows(rows_in, r_up) * scale).astype(BF16)[None]
    grad_down = (dot_rows(r_act, rows_grad) * scale).astype(BF16)[None]

    routed = dot_rows(placed, back_rows.reshape(n_rows, width))
    grad_tokens = (mine + routed).astype(BF16)
    return (grad_tokens, grad_gate, grad_up, grad_down, *own)


def solution(mesh):
    n_dp, n_expert = mesh.devices.shape
    fine = Mesh(mesh.devices.reshape(n_dp // 2, 2, n_expert // NY, NY), ("x", "core", "z", "y"))
    dp, ex = ("x", "core"), ("z", "y")
    in_specs = (
        P(ex, dp), P(ex, dp), P(ex, None), P(ex, None), P(ex, dp, None), P(ex, dp, None), P(ex, None, dp),
        P(dp, ex), P(dp, ex), P(ex, dp),
    )
    out_specs = (P(ex, dp), P(ex, dp, None), P(ex, dp, None), P(ex, None, dp), P(dp, ex), P(dp, ex), P(ex, dp))
    return jax.shard_map(shards, mesh=fine, in_specs=in_specs, out_specs=out_specs, check_vma=False)
```

time: 228 us -> 205 us (0.90)
  waiting for transfers between devices: 97.2 us -> 64.4 us
  starting transfers between devices: 47.5 us -> 53.9 us
  other arithmetic: 11.4 us -> 5.06 us
  Pallas kernels: 17.9 us -> 23.8 us
  matrix products: 13.6 us -> 16.8 us
    ppermute x29 -> x26, waiting for transfers between devices: 74.1 us -> 52.9 us  [shift(): lax.ppermute(value, axis, [(i, (i + by) % size) for i in range(size)])]
    unnamed x64 -> x24, local copies, waits for them, and re-layouts: 18.9 us -> 3.56 us
    dynamic_update_slice x5 -> x10, local copies, waits for them, and re-layouts: 0.73 us -> 11.7 us  [shards(): group = lax.dynamic_update_slice(group, part[None], (i, start, 0))]
    all_to_all x1, waiting for transfers between devices: 17.1 us -> 6.89 us  [shards(): lax.all_to_all(back.reshape(n_exp, CAP, width), ('z', 'y'), split_axis=0,...]
    add x4 -> x0, other arithmetic: 3.66 us -> none  [the longest x2 2.15 us: x_pieces(): kept + got.astype(F32)]
    all_to_all x1, starting transfers between devices: 11.4 us -> 13.9 us  [shards(): lax.all_to_all(send, ('z', 'y'), split_axis=0, concat_axis=0, tiled=True)]
    pallas_call x0 -> x4, Pallas kernels: none -> 2.46 us  [the longest x2 1.42 us: x_pieces(): pl.pallas_call(piece_kernel, out_shape=[jax.ShapeDtypeStruct((block, cols...]
    slice x2 -> x4, local copies, waits for them, and re-layouts: 0.07 us -> 2.38 us  [the longest x2 2.35 us: shards(): grd_beyond = [shift(grd_up[:far], 'y', 1), shift(grd_down[far:], 'y', -1)]]
  transfers between devices with their start and end apart: 33 -> 31, of which waited for: 17 -> 12; matrix products, arithmetic and copies ran while one was open for 12% -> 19% of each run, Pallas kernels for 5% -> 8%
where the time goes in v1:
time: 205 us; the launch traced here: 204 us
  waiting for transfers between devices  64.4 us (31%)
  starting transfers between devices  53.9 us (26%)
  local copies, waits for them, and re-layouts  25.6 us (12%)
  Pallas kernels  23.8 us (12%)
  matrix products  16.8 us (8%)
  between operations  14.1 us (7%)
  other arithmetic  5.06 us (2%)
    ppermute x26, waiting for transfers between devices, shift(): lax.ppermute(value, axis, [(i, (i + by) % size) for i in range(size)])  52.9 us
    ppermute x26, starting transfers between devices, shift(): lax.ppermute(value, axis, [(i, (i + by) % size) for i in range(size)])  30.8 us
    all_to_all x1, starting transfers between devices, shards(): lax.all_to_all(send, ('z', 'y'), split_axis=0, concat_axis=0, tiled=True)  13.9 us
    dynamic_update_slice x10, local copies, waits for them, and re-layouts, shards(): group = lax.dynamic_update_slice(group, part[None], (i, start, 0))  11.7 us
    dot_general x4, matrix products, dot_rows(): lax.dot_general(left, right, (((0,), (0,)), ((), ())), preferred_element_...  11 us
    all_to_all x1, starting transfers between devices, shards(): lax.all_to_all(back.reshape(n_exp, CAP, width), ('z', 'y'), split_axis=0,...  9.1 us
    pallas_call x1, Pallas kernels, shared_back(): pl.pallas_call(lambda *refs: back_kernel(scale, *refs), out_shape=(jax.Sh...  8.16 us
    pallas_call x1, Pallas kernels, routed_partials(): pl.pallas_call(routed_kernel, out_shape=out, grid_spec=pltpu.PrefetchScal...  7.08 us
  transfers between devices with their start and end apart: 31, of which 12 were waited for; matrix products, arithmetic and copies ran while one was open for 19% of the time, Pallas kernels for 8%

profile of v1, /device:TPU:8, one launch (start us, length us, event | category | flops | bytes accessed | tf_op | source)
XLA Modules:
  0.0 203.8 jit_solution(4604908745682929850)
XLA Ops:
  8.8 2.2 %collective-permute-start.2 = (bf16[256,896]{1,0:T(8,128)(2,1)}, bf16[256,896]{1,0:T(8,128)(2,1)S(1)}, u32[]{:S(2)}, u32[]{:S(2)}) collective-permute-start(bf16[256,896]{1,0:T(8,128)(2,1)} %param.10), channel_id=1, source_target_pairs={{0,3},{1,0},{2,1},{3,2},{4,7},{5,4},{6,5},{7,6},{8,11},{9,8},{10,9... | collective-permute-start | bytes 1376264 | tf_op jit(solution)/shard_map/ppermute | solution.py:42
  11.0 2.0 collective-permute-start.5
  18.3 2.1 %convolution_add_fusion = f32[768,896]{1,0:T(8,128)} fusion(f32[768,896]{1,0:T(8,128)S(1)} %fusion.69, pred[768,256]{1,0:T(32,128)(4,1)S(1)} %get-tuple-element.94, bf16[256,896]{1,0:T(8,128)(2,1)S(1)} %copy-done.6), kind=kOutput, calls=%fused_computation.10 | convolution fusion | flops 353009664 | bytes 6160384 | tf_op jit(solution)/shard_map/dot_general | solution.py:29
  24.6 2.6 %collective-permute-start.3 = (bf16[128,896]{1,0:T(8,128)(2,1)S(1)}, bf16[128,896]{1,0:T(8,128)(2,1)S(1)}, u32[]{:S(2)}, u32[]{:S(2)}) collective-permute-start(bf16[128,896]{1,0:T(8,128)(2,1)S(1)} %slice.152), channel_id=1, source_target_pairs={{0,3},{1,0},{2,1},{3,2},{4,7},{5,4},{6,5},{7,6},{8,11},{9,8},{10,9... | collective-permute-start | bytes 688136 | tf_op jit(solution)/shard_map/ppermute | solution.py:42
  27.2 5.1 %collective-permute-done.5 = bf16[256,896]{1,0:T(8,128)(2,1)S(1)} collective-permute-done((bf16[256,896]{1,0:T(8,128)(2,1)}, bf16[256,896]{1,0:T(8,128)(2,1)S(1)}, u32[]{:S(2)}, u32[]{:S(2)}) %collective-permute-start.5) | collective-permute-done | bytes 458784 | tf_op jit(solution)/shard_map/ppermute | solution.py:42
  36.7 1.8 bitcast_dynamic-update-slice_fusion.1
  41.6 13.9 %all-to-all-start = ((bf16[32,24,896]{2,1,0:T(8,128)(2,1)}), bf16[32,24,896]{2,1,0:T(8,128)(2,1)S(1)}, u32[]{:S(2)}, u32[]{:S(2)}) async-start(bf16[32,24,896]{2,1,0:T(8,128)(2,1)} %multiply_convert_fusion.3), calls=%async_computation | async-start | bytes 2752512 | tf_op jit(solution)/shard_map/all_to_all | solution.py:353
  55.6 1.6 bitcast_dynamic-update-slice_fusion.7
  60.3 5.4 %shared_partials.1 = (bf16[512,768]{1,0:T(8,128)(2,1)S(1)}, f32[512,768]{1,0:T(8,128)S(1)}) custom-call(s32[2]{0:T(128)S(1)} %pad_add_fusion.where, bf16[4,256,896]{2,1,0:T(8,128)(2,1)} %bitcast_dynamic-update-slice_fusion.6.tok.refs_1_, bf16[4,256,896]{2,1,0:T(8,128)(2,1)} %bitcast_dynamic-update-slice_fusion.4.grd.refs_2_, bf16[8,96,896]{2,1,0:T(8,128)(2,1)} %bitcast.134), custom_call_target="tpu_custom_call" | custom-call | flops 1409286144 | bytes 3670016 | tf_op jit(solution)/shard_map/shared_partials/pallas_call | solution.py:166
  65.9 2.3 %collective-permute-done.8.got = bf16[512,768]{1,0:T(8,128)(2,1)S(1)} collective-permute-done((bf16[512,768]{1,0:T(8,128)(2,1)S(1)}, bf16[512,768]{1,0:T(8,128)(2,1)S(1)}, u32[]{:S(2)}, u32[]{:S(2)}) %collective-permute-start.8) | collective-permute-done | bytes 786464 | tf_op jit(solution)/shard_map/ppermute | solution.py:42
  68.8 1.7 collective-permute-start.9
  70.5 2.7 %collective-permute-start.10 = (bf16[128,768]{1,0:T(8,128)(2,1)S(1)}, bf16[128,768]{1,0:T(8,128)(2,1)S(1)}, u32[]{:S(2)}, u32[]{:S(2)}) collective-permute-start(bf16[128,768]{1,0:T(8,128)(2,1)S(1)} %get-tuple-element.50), channel_id=1, source_target_pairs={{0,128},{64,192},{128,0},{192,64},{1,129},{65,193},{129,1},{193,65... | collective-permute-start | bytes 589832 | tf_op jit(solution)/shard_map/ppermute | solution.py:42
  74.7 2.5 %collective-permute-done.9.refs_0_ = bf16[128,768]{1,0:T(8,128)(2,1)S(1)} collective-permute-done((bf16[128,768]{1,0:T(8,128)(2,1)S(1)}, bf16[128,768]{1,0:T(8,128)(2,1)S(1)}, u32[]{:S(2)}, u32[]{:S(2)}) %collective-permute-start.9) | collective-permute-done | bytes 196640 | tf_op jit(solution)/shard_map/ppermute | solution.py:42
  77.2 5.2 %collective-permute-done.10.refs_1_ = bf16[128,768]{1,0:T(8,128)(2,1)S(1)} collective-permute-done((bf16[128,768]{1,0:T(8,128)(2,1)S(1)}, bf16[128,768]{1,0:T(8,128)(2,1)S(1)}, u32[]{:S(2)}, u32[]{:S(2)}) %collective-permute-start.10) | collective-permute-done | bytes 196640 | tf_op jit(solution)/shard_map/ppermute | solution.py:42
  83.3 4.5 %all-to-all-done = bf16[32,24,896]{2,1,0:T(8,128)(2,1)S(1)} async-done(((bf16[32,24,896]{2,1,0:T(8,128)(2,1)}), bf16[32,24,896]{2,1,0:T(8,128)(2,1)S(1)}, u32[]{:S(2)}, u32[]{:S(2)}) %all-to-all-start) | async-done | bytes 1376288 | tf_op jit(solution)/shard_map/all_to_all | solution.py:353
  87.8 7.1 %routed_partials.1 = (bf16[768,896]{1,0:T(8,128)(2,1)S(1)}, bf16[192,3072]{1,0:T(8,128)(2,1)S(1)}, f32[192,3072]{1,0:T(8,128)S(1)}) custom-call(s32[2]{0:T(128)S(1)} %pad_add_fusion.where, bf16[768,768]{1,0:T(8,128)(2,1)S(1)} %fusion.compact, bf16[768,896]{1,0:T(8,128)(2,1)S(1)} %bitcast.89, bf16[1,896,1024]{2,1,0:T(8,128)(2,1)} %w_gate.1, ...), custom_call_target="tpu_custom_call" | custom-call | flops 2113929216 | bytes 5505024 | tf_op jit(solution)/shard_map/routed_partials/pallas_call | solution.py:278
  95.0 2.8 %collective-permute-done.12.got = bf16[192,3072]{1,0:T(8,128)(2,1)S(1)} collective-permute-done((bf16[192,3072]{1,0:T(8,128)(2,1)S(1)}, bf16[192,3072]{1,0:T(8,128)(2,1)S(1)}, u32[]{:S(2)}, u32[]{:S(2)}) %collective-permute-start.12) | collective-permute-done | bytes 1179680 | tf_op jit(solution)/shard_map/ppermute | solution.py:42
  100.2 2.7 %collective-permute-start.14 = (bf16[48,3072]{1,0:T(8,128)(2,1)S(1)}, bf16[48,3072]{1,0:T(8,128)(2,1)S(1)}, u32[]{:S(2)}, u32[]{:S(2)}) collective-permute-start(bf16[48,3072]{1,0:T(8,128)(2,1)S(1)} %get-tuple-element.59), channel_id=1, source_target_pairs={{0,128},{64,192},{128,0},{192,64},{1,129},{65,193},{129,1},{193,65... | collective-permute-start | bytes 884744 | tf_op jit(solution)/shard_map/ppermute | solution.py:42
  104.4 8.6 %collective-permute-done.13.refs_0_ = bf16[48,3072]{1,0:T(8,128)(2,1)S(1)} collective-permute-done((bf16[48,3072]{1,0:T(8,128)(2,1)S(1)}, bf16[48,3072]{1,0:T(8,128)(2,1)S(1)}, u32[]{:S(2)}, u32[]{:S(2)}) %collective-permute-start.13) | collective-permute-done | bytes 294944 | tf_op jit(solution)/shard_map/ppermute | solution.py:42
  112.9 6.8 %collective-permute-done.14.refs_1_ = bf16[48,3072]{1,0:T(8,128)(2,1)S(1)} collective-permute-done((bf16[48,3072]{1,0:T(8,128)(2,1)S(1)}, bf16[48,3072]{1,0:T(8,128)(2,1)S(1)}, u32[]{:S(2)}, u32[]{:S(2)}) %collective-permute-start.14) | collective-permute-done | bytes 294944 | tf_op jit(solution)/shard_map/ppermute | solution.py:42
  121.4 8.2 %shared_back.1 = (f32[256,896]{1,0:T(8,128)S(1)}, bf16[4,256,896]{2,1,0:T(8,128)(2,1)S(1)}, bf16[8,96,896]{2,1,0:T(8,128)(2,1)}) custom-call(bf16[1024,768]{1,0:T(8,128)(2,1)S(1)} %copy-done.2, bf16[4,256,896]{2,1,0:T(8,128)(2,1)} %bitcast_dynamic-update-slice_fusion.6.tok.refs_1_, bf16[4,256,896]{2,1,0:T(8,128)(2,1)} %bitcast_dynamic-update-slice_fusion.4.grd.refs_2_, ...), custom_call_target="tpu_custom_call" | custom-call | flops 2348810240 | bytes 7340032 | tf_op jit(solution)/shard_map/shared_back/pallas_call | solution.py:223
  131.3 3.2 %collective-permute-start.20 = (bf16[48,3072]{1,0:T(8,128)(2,1)S(1)}, bf16[48,3072]{1,0:T(8,128)(2,1)S(1)}, u32[]{:S(2)}, u32[]{:S(2)}) collective-permute-start(bf16[48,3072]{1,0:T(8,128)(2,1)S(1)} %x_products.3.refs_0_), channel_id=1, source_target_pairs={{0,128},{64,192},{128,0},{192,64},{1,129},{65,193},{129,1},{193,65... | collective-permute-start | bytes 884744 | tf_op jit(solution)/shard_map/ppermute | solution.py:42
  134.8 6.2 %collective-permute-done.21.refs_3_ = bf16[48,3072]{1,0:T(8,128)(2,1)S(1)} collective-permute-done((bf16[48,3072]{1,0:T(8,128)(2,1)S(1)}, bf16[48,3072]{1,0:T(8,128)(2,1)S(1)}, u32[]{:S(2)}, u32[]{:S(2)}) %collective-permute-start.21) | collective-permute-done | bytes 294944 | tf_op jit(solution)/shard_map/ppermute | solution.py:42
  141.0 6.5 %collective-permute-done.20.refs_2_ = bf16[48,3072]{1,0:T(8,128)(2,1)S(1)} collective-permute-done((bf16[48,3072]{1,0:T(8,128)(2,1)S(1)}, bf16[48,3072]{1,0:T(8,128)(2,1)S(1)}, u32[]{:S(2)}, u32[]{:S(2)}) %collective-permute-start.20) | collective-permute-done | bytes 294944 | tf_op jit(solution)/shard_map/ppermute | solution.py:42
  151.2 3.3 %collective-permute-start.17 = (bf16[256,896]{1,0:T(8,128)(2,1)}, bf16[256,896]{1,0:T(8,128)(2,1)}, u32[]{:S(2)}, u32[]{:S(2)}) collective-permute-start(bf16[256,896]{1,0:T(8,128)(2,1)} %get-tuple-element.75), channel_id=1, source_target_pairs={{0,2},{1,3},{2,0},{3,1},{4,6},{5,7},{6,4},{7,5},{8,10},{9,11},{10,... | collective-permute-start | bytes 1376264 | tf_op jit(solution)/shard_map/ppermute | solution.py:42
  158.9 9.1 %all-to-all-start.1 = ((bf16[32,12,896]{2,1,0:T(8,128)(2,1)}), bf16[32,12,896]{2,1,0:T(8,128)(2,1)}, u32[]{:S(2)}, u32[]{:S(2)}) async-start(bf16[32,12,896]{2,1,0:T(8,128)(2,1)} %reshape.549), calls=%async_computation.1 | async-start | bytes 1835008 | tf_op jit(solution)/shard_map/all_to_all | solution.py:390
  168.0 6.8 %collective-permute-done.17 = bf16[256,896]{1,0:T(8,128)(2,1)} collective-permute-done((bf16[256,896]{1,0:T(8,128)(2,1)}, bf16[256,896]{1,0:T(8,128)(2,1)}, u32[]{:S(2)}, u32[]{:S(2)}) %collective-permute-start.17) | collective-permute-done | bytes 458784 | tf_op jit(solution)/shard_map/ppermute | solution.py:42
  174.8 3.6 %fusion.6 = bf16[1,896,1024]{2,1,0:T(8,128)(2,1)} fusion(bf16[384,3072]{1,0:T(8,128)(2,1)S(1)} %bitcast.92, bf16[768,896]{1,0:T(8,128)(2,1)} %copy-done.3), kind=kOutput, calls=%fused_computation.12 | convolution fusion | flops 706478080 | bytes 3309568 | tf_op jit(solution)/shard_map/dot_general | solution.py:21
  178.4 2.4 %fusion.5 = bf16[1,896,1024]{2,1,0:T(8,128)(2,1)} fusion(bf16[384,3072]{1,0:T(8,128)(2,1)S(1)} %bitcast.93, bf16[768,896]{1,0:T(8,128)(2,1)S(1)} %copy-done.4), kind=kOutput, calls=%fused_computation.11 | convolution fusion | flops 706478080 | bytes 3309568 | tf_op jit(solution)/shard_map/dot_general | solution.py:21
  180.8 2.5 %fusion.7 = bf16[1,1024,896]{2,1,0:T(8,128)(2,1)} fusion(bf16[384,3072]{1,0:T(8,128)(2,1)S(1)} %bitcast.94, bf16[768,896]{1,0:T(8,128)(2,1)S(1)} %copy-done.4), kind=kOutput, calls=%fused_computation.13 | convolution fusion | flops 706478080 | bytes 3309568 | tf_op jit(solution)/shard_map/dot_general | solution.py:21
  186.5 6.9 %all-to-all-done.1 = bf16[32,12,896]{2,1,0:T(8,128)(2,1)} async-done(((bf16[32,12,896]{2,1,0:T(8,128)(2,1)}), bf16[32,12,896]{2,1,0:T(8,128)(2,1)}, u32[]{:S(2)}, u32[]{:S(2)}) %all-to-all-start.1) | async-done | bytes 688160 | tf_op jit(solution)/shard_map/all_to_all | solution.py:390
  194.7 2.5 %add_convert_fusion = bf16[256,896]{1,0:T(8,128)(2,1)} fusion(bf16[256,896]{1,0:T(8,128)(2,1)} %collective-permute-done.18, bf16[256,896]{1,0:T(8,128)(2,1)} %collective-permute-done.17, f32[256,896]{1,0:T(8,128)S(1)} %copy-done.1, bf16[256,896]{1,0:T(8,128)(2,1)} %collective-permute-done.16, bf16[384,256]{1,0:T(8,128)(2,1)S(1)} %copy-done.10, ...), kind=kOutput, calls=%fused_computation.20 | convolution fusion | flops 177995776 | bytes 3637248 | tf_op jit(solution)/shard_map/dot_general | solution.py:21
  (117 shorter events, 44.7 us)
Async XLA Ops:
  7.2 53.1 %all-gather.3.cloned.1.call-start = ((), (), s32[]{:S(2)}) async-start(), calls=%async_computation.3 | async-start | bytes 1548288 | tf_op jit(solution)/shard_map/all_gather | solution.py:314
  8.8 15.7 %collective-permute-start.2 = (bf16[256,896]{1,0:T(8,128)(2,1)}, bf16[256,896]{1,0:T(8,128)(2,1)S(1)}, u32[]{:S(2)}, u32[]{:S(2)}) collective-permute-start(bf16[256,896]{1,0:T(8,128)(2,1)} %param.10), channel_id=1, source_target_pairs={{0,3},{1,0},{2,1},{3,2},{4,7},{5,4},{6,5},{7,6},{8,11},{9,8},{10,9... | collective-permute-start | bytes 1376264 | tf_op jit(solution)/shard_map/ppermute | solution.py:42
  11.0 16.1 %collective-permute-start = (bf16[256,896]{1,0:T(8,128)(2,1)}, bf16[256,896]{1,0:T(8,128)(2,1)S(1)}, u32[]{:S(2)}, u32[]{:S(2)}) collective-permute-start(bf16[256,896]{1,0:T(8,128)(2,1)} %param.10), channel_id=1, source_target_pairs={{0,1},{1,2},{2,3},{3,0},{4,5},{5,6},{6,7},{7,4},{8,9},{9,10},{10,1... | collective-permute-start | bytes 1376264 | tf_op jit(solution)/shard_map/ppermute | solution.py:42
  11.0 21.3 %collective-permute-start.5 = (bf16[256,896]{1,0:T(8,128)(2,1)}, bf16[256,896]{1,0:T(8,128)(2,1)S(1)}, u32[]{:S(2)}, u32[]{:S(2)}) collective-permute-start(bf16[256,896]{1,0:T(8,128)(2,1)} %param.11), channel_id=1, source_target_pairs={{0,3},{1,0},{2,1},{3,2},{4,7},{5,4},{6,5},{7,6},{8,11},{9,8},{10,9... | collective-permute-start | bytes 1376264 | tf_op jit(solution)/shard_map/ppermute | solution.py:42
  13.1 21.6 %collective-permute-start.4 = (bf16[256,896]{1,0:T(8,128)(2,1)}, bf16[256,896]{1,0:T(8,128)(2,1)}, u32[]{:S(2)}, u32[]{:S(2)}) collective-permute-start(bf16[256,896]{1,0:T(8,128)(2,1)} %param.11), channel_id=1, source_target_pairs={{0,1},{1,2},{2,3},{3,0},{4,5},{5,6},{6,7},{7,4},{8,9},{9,10},{10,1... | collective-permute-start | bytes 1376264 | tf_op jit(solution)/shard_map/ppermute | solution.py:42
  24.6 16.4 %collective-permute-start.3 = (bf16[128,896]{1,0:T(8,128)(2,1)S(1)}, bf16[128,896]{1,0:T(8,128)(2,1)S(1)}, u32[]{:S(2)}, u32[]{:S(2)}) collective-permute-start(bf16[128,896]{1,0:T(8,128)(2,1)S(1)} %slice.152), channel_id=1, source_target_pairs={{0,3},{1,0},{2,1},{3,2},{4,7},{5,4},{6,5},{7,6},{8,11},{9,8},{10,9... | collective-permute-start | bytes 688136 | tf_op jit(solution)/shard_map/ppermute | solution.py:42
  27.1 13.8 %collective-permute-start.1 = (bf16[128,896]{1,0:T(8,128)(2,1)S(1)}, bf16[128,896]{1,0:T(8,128)(2,1)S(1)}, u32[]{:S(2)}, u32[]{:S(2)}) collective-permute-start(bf16[128,896]{1,0:T(8,128)(2,1)S(1)} %slice.151), channel_id=1, source_target_pairs={{0,1},{1,2},{2,3},{3,0},{4,5},{5,6},{6,7},{7,4},{8,9},{9,10},{10,1... | collective-permute-start | bytes 688136 | tf_op jit(solution)/shard_map/ppermute | solution.py:42
  33.0 26.6 %collective-permute-start.7 = (bf16[128,896]{1,0:T(8,128)(2,1)}, bf16[128,896]{1,0:T(8,128)(2,1)S(1)}, u32[]{:S(2)}, u32[]{:S(2)}) collective-permute-start(bf16[128,896]{1,0:T(8,128)(2,1)} %slice.154), channel_id=1, source_target_pairs={{0,3},{1,0},{2,1},{3,2},{4,7},{5,4},{6,5},{7,6},{8,11},{9,8},{10,9... | collective-permute-start | bytes 688136 | tf_op jit(solution)/shard_map/ppermute | solution.py:42
  36.3 21.7 %collective-permute-start.6 = (bf16[128,896]{1,0:T(8,128)(2,1)}, bf16[128,896]{1,0:T(8,128)(2,1)}, u32[]{:S(2)}, u32[]{:S(2)}) collective-permute-start(bf16[128,896]{1,0:T(8,128)(2,1)} %slice.153), channel_id=1, source_target_pairs={{0,1},{1,2},{2,3},{3,0},{4,5},{5,6},{6,7},{7,4},{8,9},{9,10},{10,1... | collective-permute-start | bytes 688136 | tf_op jit(solution)/shard_map/ppermute | solution.py:42
  41.6 46.2 %all-to-all-start = ((bf16[32,24,896]{2,1,0:T(8,128)(2,1)}), bf16[32,24,896]{2,1,0:T(8,128)(2,1)S(1)}, u32[]{:S(2)}, u32[]{:S(2)}) async-start(bf16[32,24,896]{2,1,0:T(8,128)(2,1)} %multiply_convert_fusion.3), calls=%async_computation | async-start | bytes 2752512 | tf_op jit(solution)/shard_map/all_to_all | solution.py:353
  55.5 64.4 %all-gather.5.cloned.1.call-start = ((), (), s32[]{:S(2)}) async-start(), calls=%async_computation.4 | async-start | bytes 1769472 | tf_op jit(solution)/shard_map/all_gather | solution.py:369
  65.8 2.4 %collective-permute-start.8 = (bf16[512,768]{1,0:T(8,128)(2,1)S(1)}, bf16[512,768]{1,0:T(8,128)(2,1)S(1)}, u32[]{:S(2)}, u32[]{:S(2)}) collective-permute-start(bf16[512,768]{1,0:T(8,128)(2,1)S(1)} %get-tuple-element.47), channel_id=1, source_target_pairs={{0,32},{32,0},{1,33},{33,1},{2,34},{34,2},{3,35},{35,3},{4,36},{36... | collective-permute-start | bytes 2359304 | tf_op jit(solution)/shard_map/ppermute | solution.py:42
  68.8 8.4 %collective-permute-start.9 = (bf16[128,768]{1,0:T(8,128)(2,1)S(1)}, bf16[128,768]{1,0:T(8,128)(2,1)S(1)}, u32[]{:S(2)}, u32[]{:S(2)}) collective-permute-start(bf16[128,768]{1,0:T(8,128)(2,1)S(1)} %get-tuple-element.49), channel_id=1, source_target_pairs={{0,64},{64,128},{128,192},{192,0},{1,65},{65,129},{129,193},{193,1... | collective-permute-start | bytes 589832 | tf_op jit(solution)/shard_map/ppermute | solution.py:42
  70.5 11.9 %collective-permute-start.10 = (bf16[128,768]{1,0:T(8,128)(2,1)S(1)}, bf16[128,768]{1,0:T(8,128)(2,1)S(1)}, u32[]{:S(2)}, u32[]{:S(2)}) collective-permute-start(bf16[128,768]{1,0:T(8,128)(2,1)S(1)} %get-tuple-element.50), channel_id=1, source_target_pairs={{0,128},{64,192},{128,0},{192,64},{1,129},{65,193},{129,1},{193,65... | collective-permute-start | bytes 589832 | tf_op jit(solution)/shard_map/ppermute | solution.py:42
  73.3 9.1 %collective-permute-start.11 = (bf16[128,768]{1,0:T(8,128)(2,1)S(1)}, bf16[128,768]{1,0:T(8,128)(2,1)S(1)}, u32[]{:S(2)}, u32[]{:S(2)}) collective-permute-start(bf16[128,768]{1,0:T(8,128)(2,1)S(1)} %get-tuple-element.51), channel_id=1, source_target_pairs={{0,192},{64,0},{128,64},{192,128},{1,193},{65,1},{129,65},{193,129... | collective-permute-start | bytes 589832 | tf_op jit(solution)/shard_map/ppermute | solution.py:42
  83.3 100.0 %reduce-scatter.2.cloned.1.call-start = ((), (), s32[]{:S(2)}) async-start(), calls=%async_computation.5 | async-start | bytes 1548288 | tf_op jit(solution)/shard_map/reduce_scatter | solution.py:384
  94.9 24.8 %copy-start.3 = (bf16[768,896]{1,0:T(8,128)(2,1)}, bf16[768,896]{1,0:T(8,128)(2,1)S(1)}, u32[]{:S(2)}) copy-start(bf16[768,896]{1,0:T(8,128)(2,1)S(1)} %get-tuple-element.68) | copy-start | bytes 4128772
  94.9 2.9 %collective-permute-start.12 = (bf16[192,3072]{1,0:T(8,128)(2,1)S(1)}, bf16[192,3072]{1,0:T(8,128)(2,1)S(1)}, u32[]{:S(2)}, u32[]{:S(2)}) collective-permute-start(bf16[192,3072]{1,0:T(8,128)(2,1)S(1)} %get-tuple-element.56), channel_id=1, source_target_pairs={{0,32},{32,0},{1,33},{33,1},{2,34},{34,2},{3,35},{35,3},{4,36},{36... | collective-permute-start | bytes 3538952 | tf_op jit(solution)/shard_map/ppermute | solution.py:42
  98.6 14.3 %collective-permute-start.13 = (bf16[48,3072]{1,0:T(8,128)(2,1)S(1)}, bf16[48,3072]{1,0:T(8,128)(2,1)S(1)}, u32[]{:S(2)}, u32[]{:S(2)}) collective-permute-start(bf16[48,3072]{1,0:T(8,128)(2,1)S(1)} %get-tuple-element.58), channel_id=1, source_target_pairs={{0,64},{64,128},{128,192},{192,0},{1,65},{65,129},{129,193},{193,1... | collective-permute-start | bytes 884744 | tf_op jit(solution)/shard_map/ppermute | solution.py:42
  100.2 19.6 %collective-permute-start.14 = (bf16[48,3072]{1,0:T(8,128)(2,1)S(1)}, bf16[48,3072]{1,0:T(8,128)(2,1)S(1)}, u32[]{:S(2)}, u32[]{:S(2)}) collective-permute-start(bf16[48,3072]{1,0:T(8,128)(2,1)S(1)} %get-tuple-element.59), channel_id=1, source_target_pairs={{0,128},{64,192},{128,0},{192,64},{1,129},{65,193},{129,1},{193,65... | collective-permute-start | bytes 884744 | tf_op jit(solution)/shard_map/ppermute | solution.py:42
  102.9 16.8 %collective-permute-start.15 = (bf16[48,3072]{1,0:T(8,128)(2,1)S(1)}, bf16[48,3072]{1,0:T(8,128)(2,1)S(1)}, u32[]{:S(2)}, u32[]{:S(2)}) collective-permute-start(bf16[48,3072]{1,0:T(8,128)(2,1)S(1)} %get-tuple-element.60), channel_id=1, source_target_pairs={{0,192},{64,0},{128,64},{192,128},{1,193},{65,1},{129,65},{193,129... | collective-permute-start | bytes 884744 | tf_op jit(solution)/shard_map/ppermute | solution.py:42
  130.5 10.5 %collective-permute-start.21 = (bf16[48,3072]{1,0:T(8,128)(2,1)S(1)}, bf16[48,3072]{1,0:T(8,128)(2,1)S(1)}, u32[]{:S(2)}, u32[]{:S(2)}) collective-permute-start(bf16[48,3072]{1,0:T(8,128)(2,1)S(1)} %x_products.3.refs_0_), channel_id=1, source_target_pairs={{0,64},{64,128},{128,192},{192,0},{1,65},{65,129},{129,193},{193,1... | collective-permute-start | bytes 884744 | tf_op jit(solution)/shard_map/ppermute | solution.py:42
  131.3 16.3 %collective-permute-start.20 = (bf16[48,3072]{1,0:T(8,128)(2,1)S(1)}, bf16[48,3072]{1,0:T(8,128)(2,1)S(1)}, u32[]{:S(2)}, u32[]{:S(2)}) collective-permute-start(bf16[48,3072]{1,0:T(8,128)(2,1)S(1)} %x_products.3.refs_0_), channel_id=1, source_target_pairs={{0,128},{64,192},{128,0},{192,64},{1,129},{65,193},{129,1},{193,65... | collective-permute-start | bytes 884744 | tf_op jit(solution)/shard_map/ppermute | solution.py:42
  134.4 13.1 %collective-permute-start.19 = (bf16[48,3072]{1,0:T(8,128)(2,1)S(1)}, bf16[48,3072]{1,0:T(8,128)(2,1)S(1)}, u32[]{:S(2)}, u32[]{:S(2)}) collective-permute-start(bf16[48,3072]{1,0:T(8,128)(2,1)S(1)} %x_products.3.refs_0_), channel_id=1, source_target_pairs={{0,192},{64,0},{128,64},{192,128},{1,193},{65,1},{129,65},{193,129... | collective-permute-start | bytes 884744 | tf_op jit(solution)/shard_map/ppermute | solution.py:42
  134.8 15.0 %collective-permute-start.22 = (bf16[48,3072]{1,0:T(8,128)(2,1)S(1)}, bf16[48,3072]{1,0:T(8,128)(2,1)S(1)}, u32[]{:S(2)}, u32[]{:S(2)}) collective-permute-start(bf16[48,3072]{1,0:T(8,128)(2,1)S(1)} %x_products.3.refs_0_), channel_id=1, source_target_pairs={{0,32},{32,0},{1,33},{33,1},{2,34},{34,2},{3,35},{35,3},{4,36},{36... | collective-permute-start | bytes 884744 | tf_op jit(solution)/shard_map/ppermute | solution.py:42
  141.0 10.2 %collective-permute-start.25 = (bf16[48,3072]{1,0:T(8,128)(2,1)S(1)}, bf16[48,3072]{1,0:T(8,128)(2,1)S(1)}, u32[]{:S(2)}, u32[]{:S(2)}) collective-permute-start(bf16[48,3072]{1,0:T(8,128)(2,1)S(1)} %collective-permute-done.21.refs_3_), channel_id=1, source_target_pairs={{0,32},{32,0},{1,33},{33,1},{2,34},{34,2},{3,35},{35,3},{4,36},{36... | collective-permute-start | bytes 884744 | tf_op jit(solution)/shard_map/ppermute | solution.py:42
  147.6 7.0 %collective-permute-start.24 = (bf16[48,3072]{1,0:T(8,128)(2,1)S(1)}, bf16[48,3072]{1,0:T(8,128)(2,1)S(1)}, u32[]{:S(2)}, u32[]{:S(2)}) collective-permute-start(bf16[48,3072]{1,0:T(8,128)(2,1)S(1)} %collective-permute-done.20.refs_2_), channel_id=1, source_target_pairs={{0,32},{32,0},{1,33},{33,1},{2,34},{34,2},{3,35},{35,3},{4,36},{36... | collective-permute-start | bytes 884744 | tf_op jit(solution)/shard_map/ppermute | solution.py:42
  147.6 7.0 %collective-permute-start.23 = (bf16[48,3072]{1,0:T(8,128)(2,1)S(1)}, bf16[48,3072]{1,0:T(8,128)(2,1)S(1)}, u32[]{:S(2)}, u32[]{:S(2)}) collective-permute-start(bf16[48,3072]{1,0:T(8,128)(2,1)S(1)} %collective-permute-done.19.refs_1_), channel_id=1, source_target_pairs={{0,32},{32,0},{1,33},{33,1},{2,34},{34,2},{3,35},{35,3},{4,36},{36... | collective-permute-start | bytes 884744 | tf_op jit(solution)/shard_map/ppermute | solution.py:42
  149.2 18.8 %collective-permute-start.16 = (bf16[256,896]{1,0:T(8,128)(2,1)}, bf16[256,896]{1,0:T(8,128)(2,1)}, u32[]{:S(2)}, u32[]{:S(2)}) collective-permute-start(bf16[256,896]{1,0:T(8,128)(2,1)} %get-tuple-element.73), channel_id=1, source_target_pairs={{0,3},{1,0},{2,1},{3,2},{4,7},{5,4},{6,5},{7,6},{8,11},{9,8},{10,9... | collective-permute-start | bytes 1376264 | tf_op jit(solution)/shard_map/ppermute | solution.py:42
  149.7 18.3 %collective-permute-start.18 = (bf16[256,896]{1,0:T(8,128)(2,1)}, bf16[256,896]{1,0:T(8,128)(2,1)}, u32[]{:S(2)}, u32[]{:S(2)}) collective-permute-start(bf16[256,896]{1,0:T(8,128)(2,1)} %get-tuple-element.74), channel_id=1, source_target_pairs={{0,1},{1,2},{2,3},{3,0},{4,5},{5,6},{6,7},{7,4},{8,9},{9,10},{10,1... | collective-permute-start | bytes 1376264 | tf_op jit(solution)/shard_map/ppermute | solution.py:42
  151.2 23.6 %collective-permute-start.17 = (bf16[256,896]{1,0:T(8,128)(2,1)}, bf16[256,896]{1,0:T(8,128)(2,1)}, u32[]{:S(2)}, u32[]{:S(2)}) collective-permute-start(bf16[256,896]{1,0:T(8,128)(2,1)} %get-tuple-element.75), channel_id=1, source_target_pairs={{0,2},{1,3},{2,0},{3,1},{4,6},{5,7},{6,4},{7,5},{8,10},{9,11},{10,... | collective-permute-start | bytes 1376264 | tf_op jit(solution)/shard_map/ppermute | solution.py:42
  158.9 34.5 %all-to-all-start.1 = ((bf16[32,12,896]{2,1,0:T(8,128)(2,1)}), bf16[32,12,896]{2,1,0:T(8,128)(2,1)}, u32[]{:S(2)}, u32[]{:S(2)}) async-start(bf16[32,12,896]{2,1,0:T(8,128)(2,1)} %reshape.549), calls=%async_computation.1 | async-start | bytes 1835008 | tf_op jit(solution)/shard_map/all_to_all | solution.py:390
  (11 other events, 49.0 us)
Sparse Core Ops, SparseCore 0:
  13.2 45.6 all-gather.2
  83.4 31.9 all-gather.4
  130.6 39.7 reduce-scatter.1

commit v2 on v1

--- a/solution.py
+++ b/solution.py
@@ -188,9 +188,7 @@
     nz, units, width = weights.shape[0], weights.shape[1] // 3, weights.shape[2]
     sh = nz * units
     gate, up = (weights[:, k * units : (k + 1) * units].reshape(sh, width) for k in range(2))
-    n_tok = tok.shape[1]
-    spot = pl.ds(pl.multiple_of(step * n_tok, n_tok), n_tok)
-    act, d_gate, d_up = (products[spot, k * sh : (k + 1) * sh] for k in range(3))
+    act, d_gate, d_up = (products[:, k * sh : (k + 1) * sh] for k in range(3))
     total = dot(d_gate, gate) + dot(d_up, up)
     back[step] = total.astype(BF16)
 
@@ -229,17 +227,17 @@
         ),
         grid=(n_y,),
         scratch_shapes=[pltpu.VMEM(weights.shape, F32)],
-        in_specs=[VMEM, rows, rows, whole],
+        in_specs=[pl.BlockSpec((n_tok, cols), lambda i: (i, 0)), rows, rows, whole],
         out_specs=[VMEM, VMEM, whole],
         compiler_params=pltpu.CompilerParams(vmem_limit_bytes=16 << 20),
         cost_estimate=pl.CostEstimate(
             flops=10 * n_y * n_tok * width * cols // 3, bytes_accessed=8 * n_y * n_tok * width, transcendentals=0
         ),
         name="shared_back",
-    )(products, *(pltpu.with_memory_space_constraint(v, pltpu.HBM) for v in (tok, grd, weights)))
-
-
-def routed_kernel(where, compact, recv, w_gate, w_up, w_down, rows, send, kept):
+    )(*(pltpu.with_memory_space_constraint(v, pltpu.HBM) for v in (products, tok, grd, weights)))
+
+
+def routed_kernel(where, compact, recv, w_gate, w_up, w_down, rows, send, kept, ordered):
     step = pl.program_id(0)
     n_rows, tile = rows.shape[0] // 2, w_gate.shape[2]
     half = n_rows // 2
@@ -248,17 +246,12 @@
     @pl.when(step == 0)
     def _():
         rows[...] = dot(compact[...], recv[...]).astype(BF16)
-
-    def ordered(base):
-        return jnp.concatenate(
-            [
-                rows[pl.ds(pl.multiple_of(base + (1 - where[1]) * half, half), half)],
-                rows[pl.ds(pl.multiple_of(base + where[1] * half, half), half)],
-            ],
-            axis=0,
-        )
-
-    rows_in, rows_grad = ordered(0), ordered(n_rows)
+        for base in (0, n_rows):
+            for i, side in enumerate((1 - where[1], where[1])):
+                source = pl.ds(pl.multiple_of(base + side * half, half), half)
+                ordered[base + i * half : base + (i + 1) * half, :] = rows[source, :]
+
+    rows_in, rows_grad = ordered[:n_rows, :], ordered[n_rows:, :]
     part = [dot(rows_in, w_gate[0]), dot(rows_in, w_up[0]), dot_cols(rows_grad, w_down[0])]
     for k in range(3):
         spot = pl.ds(pl.multiple_of(k * hid + step * tile, tile), tile)
@@ -269,7 +262,7 @@
 def routed_partials(where, compact, recv, w_gate, w_up, w_down):
     n_rows = recv.shape[0] // 2
     width, hid = w_gate.shape[1:]
-    tile = min(256, hid)
+    tile = min(512, hid)
     out = [
         jax.ShapeDtypeStruct((2 * n_rows, width), BF16),
         jax.ShapeDtypeStruct((n_rows // 2, 3 * hid), BF16),
@@ -289,6 +282,7 @@
                 pl.BlockSpec((1, tile, width), lambda i, where: (0, i, 0)),
             ],
             out_specs=[VMEM] * 3,
+            scratch_shapes=[pltpu.VMEM((2 * n_rows, width), BF16)],
         ),
         compiler_params=pltpu.CompilerParams(vmem_limit_bytes=14 << 20),
         cost_estimate=pl.CostEstimate(

time: 205 us -> 204 us (level)
  transfers between devices with their start and end apart: 31 -> 31, of which waited for: 12 -> 13; matrix products, arithmetic and copies ran while one was open for 19% -> 19% of each run, Pallas kernels for 8% -> 7%
where the time goes in v2:
time: 204 us; the launch traced here: 202 us
  waiting for transfers between devices  64.8 us (32%)
  starting transfers between devices  53.5 us (26%)
  local copies, waits for them, and re-layouts  24.3 us (12%)
  Pallas kernels  23.6 us (12%)
  matrix products  16.8 us (8%)
  between operations  14.1 us (7%)
  other arithmetic  5.06 us (2%)
    ppermute x26, waiting for transfers between devices, shift(): lax.ppermute(value, axis, [(i, (i + by) % size) for i in range(size)])  53.8 us
    ppermute x26, starting transfers between devices, shift(): lax.ppermute(value, axis, [(i, (i + by) % size) for i in range(size)])  30.4 us
    all_to_all x1, starting transfers between devices, shards(): lax.all_to_all(send, ('z', 'y'), split_axis=0, concat_axis=0, tiled=True)  13.9 us
    dynamic_update_slice x10, local copies, waits for them, and re-layouts, shards(): group = lax.dynamic_update_slice(group, part[None], (i, start, 0))  11.7 us
    dot_general x4, matrix products, dot_rows(): lax.dot_general(left, right, (((0,), (0,)), ((), ())), preferred_element_...  11 us
    all_to_all x1, starting transfers between devices, shards(): lax.all_to_all(back.reshape(n_exp, CAP, width), ('z', 'y'), split_axis=0,...  8.97 us
    pallas_call x1, Pallas kernels, shared_back(): pl.pallas_call(lambda *refs: back_kernel(scale, *refs), out_shape=(jax.Sh...  8.48 us
    pallas_call x1, Pallas kernels, routed_partials(): pl.pallas_call(routed_kernel, out_shape=out, grid_spec=pltpu.PrefetchScal...  6.57 us
  transfers between devices with their start and end apart: 31, of which 13 were waited for; matrix products, arithmetic and copies ran while one was open for 19% of the time, Pallas kernels for 7%

profile of v2, /device:TPU:8, one launch (start us, length us, event | category | flops | bytes accessed | tf_op | source)
XLA Modules:
  0.0 202.2 jit_solution(16029895649663823787)
XLA Ops:
  8.8 2.2 %collective-permute-start.2 = (bf16[256,896]{1,0:T(8,128)(2,1)}, bf16[256,896]{1,0:T(8,128)(2,1)S(1)}, u32[]{:S(2)}, u32[]{:S(2)}) collective-permute-start(bf16[256,896]{1,0:T(8,128)(2,1)} %param.10), channel_id=1, source_target_pairs={{0,3},{1,0},{2,1},{3,2},{4,7},{5,4},{6,5},{7,6},{8,11},{9,8},{10,9... | collective-permute-start | bytes 1376264 | tf_op jit(solution)/shard_map/ppermute | solution.py:42
  11.0 2.0 %collective-permute-start.5 = (bf16[256,896]{1,0:T(8,128)(2,1)}, bf16[256,896]{1,0:T(8,128)(2,1)S(1)}, u32[]{:S(2)}, u32[]{:S(2)}) collective-permute-start(bf16[256,896]{1,0:T(8,128)(2,1)} %param.11), channel_id=1, source_target_pairs={{0,3},{1,0},{2,1},{3,2},{4,7},{5,4},{6,5},{7,6},{8,11},{9,8},{10,9... | collective-permute-start | bytes 1376264 | tf_op jit(solution)/shard_map/ppermute | solution.py:42
  18.3 2.1 %convolution_add_fusion = f32[768,896]{1,0:T(8,128)} fusion(f32[768,896]{1,0:T(8,128)S(1)} %fusion.69, pred[768,256]{1,0:T(32,128)(4,1)S(1)} %get-tuple-element.94, bf16[256,896]{1,0:T(8,128)(2,1)S(1)} %copy-done.5), kind=kOutput, calls=%fused_computation.10 | convolution fusion | flops 353009664 | bytes 6160384 | tf_op jit(solution)/shard_map/dot_general | solution.py:29
  24.6 2.6 %collective-permute-start.3 = (bf16[128,896]{1,0:T(8,128)(2,1)S(1)}, bf16[128,896]{1,0:T(8,128)(2,1)S(1)}, u32[]{:S(2)}, u32[]{:S(2)}) collective-permute-start(bf16[128,896]{1,0:T(8,128)(2,1)S(1)} %slice.152), channel_id=1, source_target_pairs={{0,3},{1,0},{2,1},{3,2},{4,7},{5,4},{6,5},{7,6},{8,11},{9,8},{10,9... | collective-permute-start | bytes 688136 | tf_op jit(solution)/shard_map/ppermute | solution.py:42
  27.2 5.0 %collective-permute-done.5 = bf16[256,896]{1,0:T(8,128)(2,1)S(1)} collective-permute-done((bf16[256,896]{1,0:T(8,128)(2,1)}, bf16[256,896]{1,0:T(8,128)(2,1)S(1)}, u32[]{:S(2)}, u32[]{:S(2)}) %collective-permute-start.5) | collective-permute-done | bytes 458784 | tf_op jit(solution)/shard_map/ppermute | solution.py:42
  34.6 1.7 slice.153
  36.7 1.8 bitcast_dynamic-update-slice_fusion.1
  41.6 13.9 %all-to-all-start = ((bf16[32,24,896]{2,1,0:T(8,128)(2,1)}), bf16[32,24,896]{2,1,0:T(8,128)(2,1)S(1)}, u32[]{:S(2)}, u32[]{:S(2)}) async-start(bf16[32,24,896]{2,1,0:T(8,128)(2,1)} %multiply_convert_fusion.3), calls=%async_computation | async-start | bytes 2752512 | tf_op jit(solution)/shard_map/all_to_all | solution.py:347
  60.3 5.4 %shared_partials.1 = (bf16[512,768]{1,0:T(8,128)(2,1)S(1)}, f32[512,768]{1,0:T(8,128)S(1)}) custom-call(s32[2]{0:T(128)S(1)} %pad_add_fusion.where, bf16[4,256,896]{2,1,0:T(8,128)(2,1)} %bitcast_dynamic-update-slice_fusion.6.tok.refs_1_, bf16[4,256,896]{2,1,0:T(8,128)(2,1)} %bitcast_dynamic-update-slice_fusion.4.grd.refs_2_, bf16[8,96,896]{2,1,0:T(8,128)(2,1)} %bitcast.134), custom_call_target="tpu_custom_call" | custom-call | flops 1409286144 | bytes 3670016 | tf_op jit(solution)/shard_map/shared_partials/pallas_call | solution.py:166
  65.9 2.3 %collective-permute-done.8.got = bf16[512,768]{1,0:T(8,128)(2,1)S(1)} collective-permute-done((bf16[512,768]{1,0:T(8,128)(2,1)S(1)}, bf16[512,768]{1,0:T(8,128)(2,1)S(1)}, u32[]{:S(2)}, u32[]{:S(2)}) %collective-permute-start.8) | collective-permute-done | bytes 786464 | tf_op jit(solution)/shard_map/ppermute | solution.py:42
  68.8 1.7 collective-permute-start.9
  70.6 2.7 %collective-permute-start.10 = (bf16[128,768]{1,0:T(8,128)(2,1)S(1)}, bf16[128,768]{1,0:T(8,128)(2,1)S(1)}, u32[]{:S(2)}, u32[]{:S(2)}) collective-permute-start(bf16[128,768]{1,0:T(8,128)(2,1)S(1)} %get-tuple-element.50), channel_id=1, source_target_pairs={{0,128},{64,192},{128,0},{192,64},{1,129},{65,193},{129,1},{193,65... | collective-permute-start | bytes 589832 | tf_op jit(solution)/shard_map/ppermute | solution.py:42
  74.7 2.5 %collective-permute-done.9.refs_0_ = bf16[128,768]{1,0:T(8,128)(2,1)S(1)} collective-permute-done((bf16[128,768]{1,0:T(8,128)(2,1)S(1)}, bf16[128,768]{1,0:T(8,128)(2,1)S(1)}, u32[]{:S(2)}, u32[]{:S(2)}) %collective-permute-start.9) | collective-permute-done | bytes 196640 | tf_op jit(solution)/shard_map/ppermute | solution.py:42
  77.2 5.2 %collective-permute-done.10.refs_1_ = bf16[128,768]{1,0:T(8,128)(2,1)S(1)} collective-permute-done((bf16[128,768]{1,0:T(8,128)(2,1)S(1)}, bf16[128,768]{1,0:T(8,128)(2,1)S(1)}, u32[]{:S(2)}, u32[]{:S(2)}) %collective-permute-start.10) | collective-permute-done | bytes 196640 | tf_op jit(solution)/shard_map/ppermute | solution.py:42
  83.3 4.5 %all-to-all-done = bf16[32,24,896]{2,1,0:T(8,128)(2,1)S(1)} async-done(((bf16[32,24,896]{2,1,0:T(8,128)(2,1)}), bf16[32,24,896]{2,1,0:T(8,128)(2,1)S(1)}, u32[]{:S(2)}, u32[]{:S(2)}) %all-to-all-start) | async-done | bytes 1376288 | tf_op jit(solution)/shard_map/all_to_all | solution.py:347
  87.8 6.6 %routed_partials.1 = (bf16[768,896]{1,0:T(8,128)(2,1)S(1)}, bf16[192,3072]{1,0:T(8,128)(2,1)S(1)}, f32[192,3072]{1,0:T(8,128)S(1)}) custom-call(s32[2]{0:T(128)S(1)} %pad_add_fusion.where, bf16[768,768]{1,0:T(8,128)(2,1)S(1)} %fusion.compact, bf16[768,896]{1,0:T(8,128)(2,1)S(1)} %bitcast.89, bf16[1,896,1024]{2,1,0:T(8,128)(2,1)} %w_gate.1, ...), custom_call_target="tpu_custom_call" | custom-call | flops 2113929216 | bytes 5505024 | tf_op jit(solution)/shard_map/routed_partials/pallas_call | solution.py:271
  94.5 2.8 %collective-permute-done.12.got = bf16[192,3072]{1,0:T(8,128)(2,1)S(1)} collective-permute-done((bf16[192,3072]{1,0:T(8,128)(2,1)S(1)}, bf16[192,3072]{1,0:T(8,128)(2,1)S(1)}, u32[]{:S(2)}, u32[]{:S(2)}) %collective-permute-start.12) | collective-permute-done | bytes 1179680 | tf_op jit(solution)/shard_map/ppermute | solution.py:42
  99.7 2.7 %collective-permute-start.14 = (bf16[48,3072]{1,0:T(8,128)(2,1)S(1)}, bf16[48,3072]{1,0:T(8,128)(2,1)S(1)}, u32[]{:S(2)}, u32[]{:S(2)}) collective-permute-start(bf16[48,3072]{1,0:T(8,128)(2,1)S(1)} %get-tuple-element.59), channel_id=1, source_target_pairs={{0,128},{64,192},{128,0},{192,64},{1,129},{65,193},{129,1},{193,65... | collective-permute-start | bytes 884744 | tf_op jit(solution)/shard_map/ppermute | solution.py:42
  103.9 8.8 %collective-permute-done.13.refs_0_ = bf16[48,3072]{1,0:T(8,128)(2,1)S(1)} collective-permute-done((bf16[48,3072]{1,0:T(8,128)(2,1)S(1)}, bf16[48,3072]{1,0:T(8,128)(2,1)S(1)}, u32[]{:S(2)}, u32[]{:S(2)}) %collective-permute-start.13) | collective-permute-done | bytes 294944 | tf_op jit(solution)/shard_map/ppermute | solution.py:42
  112.7 7.0 %collective-permute-done.14.refs_1_ = bf16[48,3072]{1,0:T(8,128)(2,1)S(1)} collective-permute-done((bf16[48,3072]{1,0:T(8,128)(2,1)S(1)}, bf16[48,3072]{1,0:T(8,128)(2,1)S(1)}, u32[]{:S(2)}, u32[]{:S(2)}) %collective-permute-start.14) | collective-permute-done | bytes 294944 | tf_op jit(solution)/shard_map/ppermute | solution.py:42
  119.9 8.5 %shared_back.1 = (f32[256,896]{1,0:T(8,128)S(1)}, bf16[4,256,896]{2,1,0:T(8,128)(2,1)S(1)}, bf16[8,96,896]{2,1,0:T(8,128)(2,1)}) custom-call(bf16[1024,768]{1,0:T(8,128)(2,1)} %all-gather.5.cloned.1.call-done.refs_0_, bf16[4,256,896]{2,1,0:T(8,128)(2,1)} %bitcast_dynamic-update-slice_fusion.6.tok.refs_1_, ...), custom_call_target="tpu_custom_call" | custom-call | flops 2348810240 | bytes 7340032 | tf_op jit(solution)/shard_map/shared_back/pallas_call | solution.py:221
  130.1 3.0 %collective-permute-start.20 = (bf16[48,3072]{1,0:T(8,128)(2,1)S(1)}, bf16[48,3072]{1,0:T(8,128)(2,1)S(1)}, u32[]{:S(2)}, u32[]{:S(2)}) collective-permute-start(bf16[48,3072]{1,0:T(8,128)(2,1)S(1)} %x_products.3.refs_0_), channel_id=1, source_target_pairs={{0,128},{64,192},{128,0},{192,64},{1,129},{65,193},{129,1},{193,65... | collective-permute-start | bytes 884744 | tf_op jit(solution)/shard_map/ppermute | solution.py:42
  133.6 6.6 %collective-permute-done.21.refs_3_ = bf16[48,3072]{1,0:T(8,128)(2,1)S(1)} collective-permute-done((bf16[48,3072]{1,0:T(8,128)(2,1)S(1)}, bf16[48,3072]{1,0:T(8,128)(2,1)S(1)}, u32[]{:S(2)}, u32[]{:S(2)}) %collective-permute-start.21) | collective-permute-done | bytes 294944 | tf_op jit(solution)/shard_map/ppermute | solution.py:42
  140.2 6.0 %collective-permute-done.20.refs_2_ = bf16[48,3072]{1,0:T(8,128)(2,1)S(1)} collective-permute-done((bf16[48,3072]{1,0:T(8,128)(2,1)S(1)}, bf16[48,3072]{1,0:T(8,128)(2,1)S(1)}, u32[]{:S(2)}, u32[]{:S(2)}) %collective-permute-start.20) | collective-permute-done | bytes 294944 | tf_op jit(solution)/shard_map/ppermute | solution.py:42
  149.9 3.2 %collective-permute-start.17 = (bf16[256,896]{1,0:T(8,128)(2,1)}, bf16[256,896]{1,0:T(8,128)(2,1)}, u32[]{:S(2)}, u32[]{:S(2)}) collective-permute-start(bf16[256,896]{1,0:T(8,128)(2,1)} %get-tuple-element.75), channel_id=1, source_target_pairs={{0,2},{1,3},{2,0},{3,1},{4,6},{5,7},{6,4},{7,5},{8,10},{9,11},{10,... | collective-permute-start | bytes 1376264 | tf_op jit(solution)/shard_map/ppermute | solution.py:42
  157.5 9.0 %all-to-all-start.1 = ((bf16[32,12,896]{2,1,0:T(8,128)(2,1)}), bf16[32,12,896]{2,1,0:T(8,128)(2,1)}, u32[]{:S(2)}, u32[]{:S(2)}) async-start(bf16[32,12,896]{2,1,0:T(8,128)(2,1)} %reshape.549), calls=%async_computation.1 | async-start | bytes 1835008 | tf_op jit(solution)/shard_map/all_to_all | solution.py:384
  166.5 7.2 %collective-permute-done.17 = bf16[256,896]{1,0:T(8,128)(2,1)} collective-permute-done((bf16[256,896]{1,0:T(8,128)(2,1)}, bf16[256,896]{1,0:T(8,128)(2,1)}, u32[]{:S(2)}, u32[]{:S(2)}) %collective-permute-start.17) | collective-permute-done | bytes 458784 | tf_op jit(solution)/shard_map/ppermute | solution.py:42
  173.7 3.6 %fusion.6 = bf16[1,896,1024]{2,1,0:T(8,128)(2,1)} fusion(bf16[384,3072]{1,0:T(8,128)(2,1)S(1)} %bitcast.92, bf16[768,896]{1,0:T(8,128)(2,1)} %copy-done.2), kind=kOutput, calls=%fused_computation.12 | convolution fusion | flops 706478080 | bytes 3309568 | tf_op jit(solution)/shard_map/dot_general | solution.py:21
  177.3 2.4 %fusion.5 = bf16[1,896,1024]{2,1,0:T(8,128)(2,1)} fusion(bf16[384,3072]{1,0:T(8,128)(2,1)S(1)} %bitcast.93, bf16[768,896]{1,0:T(8,128)(2,1)S(1)} %copy-done.3), kind=kOutput, calls=%fused_computation.11 | convolution fusion | flops 706478080 | bytes 3309568 | tf_op jit(solution)/shard_map/dot_general | solution.py:21
  179.7 2.5 %fusion.7 = bf16[1,1024,896]{2,1,0:T(8,128)(2,1)} fusion(bf16[384,3072]{1,0:T(8,128)(2,1)S(1)} %bitcast.94, bf16[768,896]{1,0:T(8,128)(2,1)S(1)} %copy-done.3), kind=kOutput, calls=%fused_computation.13 | convolution fusion | flops 706478080 | bytes 3309568 | tf_op jit(solution)/shard_map/dot_general | solution.py:21
  185.4 6.4 %all-to-all-done.1 = bf16[32,12,896]{2,1,0:T(8,128)(2,1)} async-done(((bf16[32,12,896]{2,1,0:T(8,128)(2,1)}), bf16[32,12,896]{2,1,0:T(8,128)(2,1)}, u32[]{:S(2)}, u32[]{:S(2)}) %all-to-all-start.1) | async-done | bytes 688160 | tf_op jit(solution)/shard_map/all_to_all | solution.py:384
  193.1 2.5 %add_convert_fusion = bf16[256,896]{1,0:T(8,128)(2,1)} fusion(bf16[256,896]{1,0:T(8,128)(2,1)} %collective-permute-done.18, bf16[256,896]{1,0:T(8,128)(2,1)} %collective-permute-done.17, f32[256,896]{1,0:T(8,128)S(1)} %copy-done.1, bf16[256,896]{1,0:T(8,128)(2,1)} %collective-permute-done.16, bf16[384,256]{1,0:T(8,128)(2,1)S(1)} %copy-done.9, ...), kind=kOutput, calls=%fused_computation.20 | convolution fusion | flops 177995776 | bytes 3637248 | tf_op jit(solution)/shard_map/dot_general | solution.py:21
  (115 shorter events, 43.4 us)
Async XLA Ops:
  7.2 53.1 %all-gather.3.cloned.1.call-start = ((), (), s32[]{:S(2)}) async-start(), calls=%async_computation.3 | async-start | bytes 1548288 | tf_op jit(solution)/shard_map/all_gather | solution.py:308
  8.8 15.7 %collective-permute-start.2 = (bf16[256,896]{1,0:T(8,128)(2,1)}, bf16[256,896]{1,0:T(8,128)(2,1)S(1)}, u32[]{:S(2)}, u32[]{:S(2)}) collective-permute-start(bf16[256,896]{1,0:T(8,128)(2,1)} %param.10), channel_id=1, source_target_pairs={{0,3},{1,0},{2,1},{3,2},{4,7},{5,4},{6,5},{7,6},{8,11},{9,8},{10,9... | collective-permute-start | bytes 1376264 | tf_op jit(solution)/shard_map/ppermute | solution.py:42
  11.0 16.1 %collective-permute-start = (bf16[256,896]{1,0:T(8,128)(2,1)}, bf16[256,896]{1,0:T(8,128)(2,1)S(1)}, u32[]{:S(2)}, u32[]{:S(2)}) collective-permute-start(bf16[256,896]{1,0:T(8,128)(2,1)} %param.10), channel_id=1, source_target_pairs={{0,1},{1,2},{2,3},{3,0},{4,5},{5,6},{6,7},{7,4},{8,9},{9,10},{10,1... | collective-permute-start | bytes 1376264 | tf_op jit(solution)/shard_map/ppermute | solution.py:42
  11.0 21.3 %collective-permute-start.5 = (bf16[256,896]{1,0:T(8,128)(2,1)}, bf16[256,896]{1,0:T(8,128)(2,1)S(1)}, u32[]{:S(2)}, u32[]{:S(2)}) collective-permute-start(bf16[256,896]{1,0:T(8,128)(2,1)} %param.11), channel_id=1, source_target_pairs={{0,3},{1,0},{2,1},{3,2},{4,7},{5,4},{6,5},{7,6},{8,11},{9,8},{10,9... | collective-permute-start | bytes 1376264 | tf_op jit(solution)/shard_map/ppermute | solution.py:42
  13.1 21.6 %collective-permute-start.4 = (bf16[256,896]{1,0:T(8,128)(2,1)}, bf16[256,896]{1,0:T(8,128)(2,1)}, u32[]{:S(2)}, u32[]{:S(2)}) collective-permute-start(bf16[256,896]{1,0:T(8,128)(2,1)} %param.11), channel_id=1, source_target_pairs={{0,1},{1,2},{2,3},{3,0},{4,5},{5,6},{6,7},{7,4},{8,9},{9,10},{10,1... | collective-permute-start | bytes 1376264 | tf_op jit(solution)/shard_map/ppermute | solution.py:42
  24.6 16.4 %collective-permute-start.3 = (bf16[128,896]{1,0:T(8,128)(2,1)S(1)}, bf16[128,896]{1,0:T(8,128)(2,1)S(1)}, u32[]{:S(2)}, u32[]{:S(2)}) collective-permute-start(bf16[128,896]{1,0:T(8,128)(2,1)S(1)} %slice.152), channel_id=1, source_target_pairs={{0,3},{1,0},{2,1},{3,2},{4,7},{5,4},{6,5},{7,6},{8,11},{9,8},{10,9... | collective-permute-start | bytes 688136 | tf_op jit(solution)/shard_map/ppermute | solution.py:42
  27.2 13.8 %collective-permute-start.1 = (bf16[128,896]{1,0:T(8,128)(2,1)S(1)}, bf16[128,896]{1,0:T(8,128)(2,1)S(1)}, u32[]{:S(2)}, u32[]{:S(2)}) collective-permute-start(bf16[128,896]{1,0:T(8,128)(2,1)S(1)} %slice.151), channel_id=1, source_target_pairs={{0,1},{1,2},{2,3},{3,0},{4,5},{5,6},{6,7},{7,4},{8,9},{9,10},{10,1... | collective-permute-start | bytes 688136 | tf_op jit(solution)/shard_map/ppermute | solution.py:42
  33.0 26.6 %collective-permute-start.7 = (bf16[128,896]{1,0:T(8,128)(2,1)}, bf16[128,896]{1,0:T(8,128)(2,1)S(1)}, u32[]{:S(2)}, u32[]{:S(2)}) collective-permute-start(bf16[128,896]{1,0:T(8,128)(2,1)} %slice.154), channel_id=1, source_target_pairs={{0,3},{1,0},{2,1},{3,2},{4,7},{5,4},{6,5},{7,6},{8,11},{9,8},{10,9... | collective-permute-start | bytes 688136 | tf_op jit(solution)/shard_map/ppermute | solution.py:42
  36.3 21.7 %collective-permute-start.6 = (bf16[128,896]{1,0:T(8,128)(2,1)}, bf16[128,896]{1,0:T(8,128)(2,1)}, u32[]{:S(2)}, u32[]{:S(2)}) collective-permute-start(bf16[128,896]{1,0:T(8,128)(2,1)} %slice.153), channel_id=1, source_target_pairs={{0,1},{1,2},{2,3},{3,0},{4,5},{5,6},{6,7},{7,4},{8,9},{9,10},{10,1... | collective-permute-start | bytes 688136 | tf_op jit(solution)/shard_map/ppermute | solution.py:42
  41.6 46.2 %all-to-all-start = ((bf16[32,24,896]{2,1,0:T(8,128)(2,1)}), bf16[32,24,896]{2,1,0:T(8,128)(2,1)S(1)}, u32[]{:S(2)}, u32[]{:S(2)}) async-start(bf16[32,24,896]{2,1,0:T(8,128)(2,1)} %multiply_convert_fusion.3), calls=%async_computation | async-start | bytes 2752512 | tf_op jit(solution)/shard_map/all_to_all | solution.py:347
  55.6 64.3 %all-gather.5.cloned.1.call-start = ((), (), s32[]{:S(2)}) async-start(), calls=%async_computation.4 | async-start | bytes 1769472 | tf_op jit(solution)/shard_map/all_gather | solution.py:363
  65.8 2.4 %collective-permute-start.8 = (bf16[512,768]{1,0:T(8,128)(2,1)S(1)}, bf16[512,768]{1,0:T(8,128)(2,1)S(1)}, u32[]{:S(2)}, u32[]{:S(2)}) collective-permute-start(bf16[512,768]{1,0:T(8,128)(2,1)S(1)} %get-tuple-element.47), channel_id=1, source_target_pairs={{0,32},{32,0},{1,33},{33,1},{2,34},{34,2},{3,35},{35,3},{4,36},{36... | collective-permute-start | bytes 2359304 | tf_op jit(solution)/shard_map/ppermute | solution.py:42
  68.8 8.4 %collective-permute-start.9 = (bf16[128,768]{1,0:T(8,128)(2,1)S(1)}, bf16[128,768]{1,0:T(8,128)(2,1)S(1)}, u32[]{:S(2)}, u32[]{:S(2)}) collective-permute-start(bf16[128,768]{1,0:T(8,128)(2,1)S(1)} %get-tuple-element.49), channel_id=1, source_target_pairs={{0,64},{64,128},{128,192},{192,0},{1,65},{65,129},{129,193},{193,1... | collective-permute-start | bytes 589832 | tf_op jit(solution)/shard_map/ppermute | solution.py:42
  70.6 11.9 %collective-permute-start.10 = (bf16[128,768]{1,0:T(8,128)(2,1)S(1)}, bf16[128,768]{1,0:T(8,128)(2,1)S(1)}, u32[]{:S(2)}, u32[]{:S(2)}) collective-permute-start(bf16[128,768]{1,0:T(8,128)(2,1)S(1)} %get-tuple-element.50), channel_id=1, source_target_pairs={{0,128},{64,192},{128,0},{192,64},{1,129},{65,193},{129,1},{193,65... | collective-permute-start | bytes 589832 | tf_op jit(solution)/shard_map/ppermute | solution.py:42
  73.3 9.1 %collective-permute-start.11 = (bf16[128,768]{1,0:T(8,128)(2,1)S(1)}, bf16[128,768]{1,0:T(8,128)(2,1)S(1)}, u32[]{:S(2)}, u32[]{:S(2)}) collective-permute-start(bf16[128,768]{1,0:T(8,128)(2,1)S(1)} %get-tuple-element.51), channel_id=1, source_target_pairs={{0,192},{64,0},{128,64},{192,128},{1,193},{65,1},{129,65},{193,129... | collective-permute-start | bytes 589832 | tf_op jit(solution)/shard_map/ppermute | solution.py:42
  83.3 98.9 %reduce-scatter.2.cloned.1.call-start = ((), (), s32[]{:S(2)}) async-start(), calls=%async_computation.5 | async-start | bytes 1548288 | tf_op jit(solution)/shard_map/reduce_scatter | solution.py:378
  94.4 25.2 %copy-start.2 = (bf16[768,896]{1,0:T(8,128)(2,1)}, bf16[768,896]{1,0:T(8,128)(2,1)S(1)}, u32[]{:S(2)}) copy-start(bf16[768,896]{1,0:T(8,128)(2,1)S(1)} %get-tuple-element.68) | copy-start | bytes 4128772
  94.4 2.9 %collective-permute-start.12 = (bf16[192,3072]{1,0:T(8,128)(2,1)S(1)}, bf16[192,3072]{1,0:T(8,128)(2,1)S(1)}, u32[]{:S(2)}, u32[]{:S(2)}) collective-permute-start(bf16[192,3072]{1,0:T(8,128)(2,1)S(1)} %get-tuple-element.56), channel_id=1, source_target_pairs={{0,32},{32,0},{1,33},{33,1},{2,34},{34,2},{3,35},{35,3},{4,36},{36... | collective-permute-start | bytes 3538952 | tf_op jit(solution)/shard_map/ppermute | solution.py:42
  98.1 14.6 %collective-permute-start.13 = (bf16[48,3072]{1,0:T(8,128)(2,1)S(1)}, bf16[48,3072]{1,0:T(8,128)(2,1)S(1)}, u32[]{:S(2)}, u32[]{:S(2)}) collective-permute-start(bf16[48,3072]{1,0:T(8,128)(2,1)S(1)} %get-tuple-element.58), channel_id=1, source_target_pairs={{0,64},{64,128},{128,192},{192,0},{1,65},{65,129},{129,193},{193,1... | collective-permute-start | bytes 884744 | tf_op jit(solution)/shard_map/ppermute | solution.py:42
  99.7 20.0 %collective-permute-start.14 = (bf16[48,3072]{1,0:T(8,128)(2,1)S(1)}, bf16[48,3072]{1,0:T(8,128)(2,1)S(1)}, u32[]{:S(2)}, u32[]{:S(2)}) collective-permute-start(bf16[48,3072]{1,0:T(8,128)(2,1)S(1)} %get-tuple-element.59), channel_id=1, source_target_pairs={{0,128},{64,192},{128,0},{192,64},{1,129},{65,193},{129,1},{193,65... | collective-permute-start | bytes 884744 | tf_op jit(solution)/shard_map/ppermute | solution.py:42
  102.4 17.2 %collective-permute-start.15 = (bf16[48,3072]{1,0:T(8,128)(2,1)S(1)}, bf16[48,3072]{1,0:T(8,128)(2,1)S(1)}, u32[]{:S(2)}, u32[]{:S(2)}) collective-permute-start(bf16[48,3072]{1,0:T(8,128)(2,1)S(1)} %get-tuple-element.60), channel_id=1, source_target_pairs={{0,192},{64,0},{128,64},{192,128},{1,193},{65,1},{129,65},{193,129... | collective-permute-start | bytes 884744 | tf_op jit(solution)/shard_map/ppermute | solution.py:42
  129.4 10.8 %collective-permute-start.21 = (bf16[48,3072]{1,0:T(8,128)(2,1)S(1)}, bf16[48,3072]{1,0:T(8,128)(2,1)S(1)}, u32[]{:S(2)}, u32[]{:S(2)}) collective-permute-start(bf16[48,3072]{1,0:T(8,128)(2,1)S(1)} %x_products.3.refs_0_), channel_id=1, source_target_pairs={{0,64},{64,128},{128,192},{192,0},{1,65},{65,129},{129,193},{193,1... | collective-permute-start | bytes 884744 | tf_op jit(solution)/shard_map/ppermute | solution.py:42
  130.1 16.1 %collective-permute-start.20 = (bf16[48,3072]{1,0:T(8,128)(2,1)S(1)}, bf16[48,3072]{1,0:T(8,128)(2,1)S(1)}, u32[]{:S(2)}, u32[]{:S(2)}) collective-permute-start(bf16[48,3072]{1,0:T(8,128)(2,1)S(1)} %x_products.3.refs_0_), channel_id=1, source_target_pairs={{0,128},{64,192},{128,0},{192,64},{1,129},{65,193},{129,1},{193,65... | collective-permute-start | bytes 884744 | tf_op jit(solution)/shard_map/ppermute | solution.py:42
  133.1 13.3 %collective-permute-start.19 = (bf16[48,3072]{1,0:T(8,128)(2,1)S(1)}, bf16[48,3072]{1,0:T(8,128)(2,1)S(1)}, u32[]{:S(2)}, u32[]{:S(2)}) collective-permute-start(bf16[48,3072]{1,0:T(8,128)(2,1)S(1)} %x_products.3.refs_0_), channel_id=1, source_target_pairs={{0,192},{64,0},{128,64},{192,128},{1,193},{65,1},{129,65},{193,129... | collective-permute-start | bytes 884744 | tf_op jit(solution)/shard_map/ppermute | solution.py:42
  133.6 14.8 %collective-permute-start.22 = (bf16[48,3072]{1,0:T(8,128)(2,1)S(1)}, bf16[48,3072]{1,0:T(8,128)(2,1)S(1)}, u32[]{:S(2)}, u32[]{:S(2)}) collective-permute-start(bf16[48,3072]{1,0:T(8,128)(2,1)S(1)} %x_products.3.refs_0_), channel_id=1, source_target_pairs={{0,32},{32,0},{1,33},{33,1},{2,34},{34,2},{3,35},{35,3},{4,36},{36... | collective-permute-start | bytes 884744 | tf_op jit(solution)/shard_map/ppermute | solution.py:42
  140.2 9.7 %collective-permute-start.25 = (bf16[48,3072]{1,0:T(8,128)(2,1)S(1)}, bf16[48,3072]{1,0:T(8,128)(2,1)S(1)}, u32[]{:S(2)}, u32[]{:S(2)}) collective-permute-start(bf16[48,3072]{1,0:T(8,128)(2,1)S(1)} %collective-permute-done.21.refs_3_), channel_id=1, source_target_pairs={{0,32},{32,0},{1,33},{33,1},{2,34},{34,2},{3,35},{35,3},{4,36},{36... | collective-permute-start | bytes 884744 | tf_op jit(solution)/shard_map/ppermute | solution.py:42
  146.2 6.9 %collective-permute-start.24 = (bf16[48,3072]{1,0:T(8,128)(2,1)S(1)}, bf16[48,3072]{1,0:T(8,128)(2,1)S(1)}, u32[]{:S(2)}, u32[]{:S(2)}) collective-permute-start(bf16[48,3072]{1,0:T(8,128)(2,1)S(1)} %collective-permute-done.20.refs_2_), channel_id=1, source_target_pairs={{0,32},{32,0},{1,33},{33,1},{2,34},{34,2},{3,35},{35,3},{4,36},{36... | collective-permute-start | bytes 884744 | tf_op jit(solution)/shard_map/ppermute | solution.py:42
  146.4 6.7 %collective-permute-start.23 = (bf16[48,3072]{1,0:T(8,128)(2,1)S(1)}, bf16[48,3072]{1,0:T(8,128)(2,1)S(1)}, u32[]{:S(2)}, u32[]{:S(2)}) collective-permute-start(bf16[48,3072]{1,0:T(8,128)(2,1)S(1)} %collective-permute-done.19.refs_1_), channel_id=1, source_target_pairs={{0,32},{32,0},{1,33},{33,1},{2,34},{34,2},{3,35},{35,3},{4,36},{36... | collective-permute-start | bytes 884744 | tf_op jit(solution)/shard_map/ppermute | solution.py:42
  147.8 18.6 %collective-permute-start.16 = (bf16[256,896]{1,0:T(8,128)(2,1)}, bf16[256,896]{1,0:T(8,128)(2,1)}, u32[]{:S(2)}, u32[]{:S(2)}) collective-permute-start(bf16[256,896]{1,0:T(8,128)(2,1)} %get-tuple-element.73), channel_id=1, source_target_pairs={{0,3},{1,0},{2,1},{3,2},{4,7},{5,4},{6,5},{7,6},{8,11},{9,8},{10,9... | collective-permute-start | bytes 1376264 | tf_op jit(solution)/shard_map/ppermute | solution.py:42
  148.4 18.1 %collective-permute-start.18 = (bf16[256,896]{1,0:T(8,128)(2,1)}, bf16[256,896]{1,0:T(8,128)(2,1)}, u32[]{:S(2)}, u32[]{:S(2)}) collective-permute-start(bf16[256,896]{1,0:T(8,128)(2,1)} %get-tuple-element.74), channel_id=1, source_target_pairs={{0,1},{1,2},{2,3},{3,0},{4,5},{5,6},{6,7},{7,4},{8,9},{9,10},{10,1... | collective-permute-start | bytes 1376264 | tf_op jit(solution)/shard_map/ppermute | solution.py:42
  149.9 23.9 %collective-permute-start.17 = (bf16[256,896]{1,0:T(8,128)(2,1)}, bf16[256,896]{1,0:T(8,128)(2,1)}, u32[]{:S(2)}, u32[]{:S(2)}) collective-permute-start(bf16[256,896]{1,0:T(8,128)(2,1)} %get-tuple-element.75), channel_id=1, source_target_pairs={{0,2},{1,3},{2,0},{3,1},{4,6},{5,7},{6,4},{7,5},{8,10},{9,11},{10,... | collective-permute-start | bytes 1376264 | tf_op jit(solution)/shard_map/ppermute | solution.py:42
  157.5 34.3 %all-to-all-start.1 = ((bf16[32,12,896]{2,1,0:T(8,128)(2,1)}), bf16[32,12,896]{2,1,0:T(8,128)(2,1)}, u32[]{:S(2)}, u32[]{:S(2)}) async-start(bf16[32,12,896]{2,1,0:T(8,128)(2,1)} %reshape.549), calls=%async_computation.1 | async-start | bytes 1835008 | tf_op jit(solution)/shard_map/all_to_all | solution.py:384
  (10 other events, 46.5 us)
Sparse Core Ops, SparseCore 0:
  13.2 45.6 all-gather.2
  83.4 34.2 all-gather.4
  129.5 39.3 reduce-scatter.1
